TPU v7x, 128 devices: a whole 4x4x4 slice. The times are simulated.
128 devices in a mesh: section: 4 (over y), seq: 16 (over x, z_hi, core), dp: 2 (over z_lo).
Axes of the slice: x: 4, y: 4, z: 4 (z_hi: 2, z_lo: 2; z = z_hi * 2 + z_lo), core: 2. Of those that a mesh axis runs over, the one named last changes fastest.
Arguments:
- roles: int32 [4], replicated, may hold values from 0 to 3, each once
- block_ids: int32 [2, 2, 3072], P(None, 'dp'), may hold values from 0 to 31, never falling along the last dimension, each value on 1 to 384 neighbouring positions
- latent: bfloat16 [2, 3072, 2560], P('dp', 'seq'), may hold values from -6 to 6
- pending: bfloat16 [2, 3072, 2560], P('dp', 'seq'), may hold values from -6 to 6
- context: float32 [2, 2560], P('dp'), may hold values from -6 to 6
- w_qkv: bfloat16 [3, 2560, 6144], P(None, None, 'seq'), may hold values from -3.3796842 to 3.3796842
- w_out: bfloat16 [3, 2048, 2560], P(None, 'seq'), may hold values from -0.125 to 0.125
- stored_attn: bfloat16 [2, 3072, 2048], P('dp', None, 'seq'), may hold values from -1.5 to 1.5
Outputs:
- block_out: bfloat16 [4, 2, 3072, 2560], P('section', 'dp', 'seq')
- dmd_grad: float32 [2, 3072, 2560], P('dp', 'seq')
- grad_out: float32 [2048, 2560], P('seq')
Inputs may be any that keep to these rules, and one draw needn't show every extreme that they name: `roles`: each section has a different role: 0 generator, 1 teacher with context, 2 teacher without context, 3 fake-score model. `block_ids`: never falling along frames, starting at 0; each block has 1 to 384 frames, and one block of each row has exactly 384.
All inputs are finite; a program needn't handle non-finite values.
Results may differ from a plain program's by a relative error of at most 0.0083.
Values may be sent and summed in bfloat16 or wider, within the bound.
No kernel may reach another device: no remote copies, remote signals or barrier semaphores. Data moves between devices by JAX's collectives and lax.ppermute only.
A program may use at most 128 MiB of HBM per device.

v0:
```python
import jax
import jax.numpy as jnp
from jax import lax
from jax.sharding import PartitionSpec as P

HEAD_DIM = 128


GUIDE = 3.0
EPSILON = 1e-06
NEGATIVE = -1e30


def attend(qkv_rows, frame_ids):
    length = qkv_rows.shape[0]
    heads_here = qkv_rows.shape[1] // (3 * HEAD_DIM)
    split = qkv_rows.reshape(length, heads_here, 3, HEAD_DIM).transpose(1, 2, 0, 3)
    block_size = min(512, length)
    block_count = length // block_size
    scale = HEAD_DIM ** (-0.5)

    def per_head(triple):
        queries = triple[0]
        keys_all = triple[1]
        values = triple[2]

        def per_block(args):
            query_rows, query_ids = args
            scores = (
                lax.dot_general(
                    query_rows,
                    keys_all,
                    (((1,), (1,)), ((), ())),
                    preferred_element_type=jnp.float32,
                )
                * scale
            )
            visible = frame_ids[None, :] <= query_ids[:, None]
            scores = jnp.where(visible, scores, NEGATIVE)
            highest = jnp.max(scores, axis=1, keepdims=True)
            expon = jnp.where(visible, jnp.exp(scores - highest), 0.0)
            probs = (expon / jnp.sum(expon, axis=1, keepdims=True)).astype(jnp.bfloat16)
            return jnp.dot(probs, values, preferred_element_type=jnp.float32).astype(jnp.bfloat16)

        blocks = lax.map(
            per_block,
            (
                queries.reshape(block_count, block_size, HEAD_DIM),
                frame_ids.reshape(block_count, block_size),
            ),
        )
        return blocks.reshape(length, HEAD_DIM)

    heads_out = lax.map(per_head, split)
    return heads_out.transpose(1, 0, 2).reshape(length, heads_here * HEAD_DIM)


def per_device(roles, block_ids, latent, pending, context, w_qkv, w_out, stored_attn):
    section = lax.axis_index("section")
    places = jnp.arange(4, dtype=jnp.int32)
    weight_table = jnp.array([0.0, -GUIDE, GUIDE - 1.0, 1.0], jnp.float32)
    section_role = jnp.sum(jnp.where(places == section, roles, 0))
    model_index = jnp.sum(jnp.where(places == section_role, jnp.array([0, 1, 1, 2], jnp.int32), 0))
    w_in = lax.dynamic_index_in_dim(w_qkv, model_index, 0, keepdims=False)
    w_proj = lax.dynamic_index_in_dim(w_out, model_index, 0, keepdims=False)
    is_generator = section_role == 0
    with_context = jnp.logical_or(section_role == 1, section_role == 3).astype(jnp.float32)
    width = latent.shape[2]
    scored = pending[0].astype(jnp.float32) + with_context * context[0][None, :]
    source = jnp.where(is_generator, latent[0].astype(jnp.float32), scored)
    normed = (
        source * lax.rsqrt(jnp.mean(source * source, axis=1, keepdims=True) + EPSILON)
    ).astype(jnp.bfloat16)
    qkv_rows = jnp.dot(
        lax.all_gather(normed, "seq", axis=0, tiled=True), w_in, preferred_element_type=jnp.float32
    ).astype(jnp.bfloat16)
    frame_ids = jnp.where(is_generator, block_ids[0, 0], block_ids[1, 0])
    attn = attend(qkv_rows, frame_ids)
    local_attn = lax.all_to_all(attn, "seq", split_axis=0, concat_axis=1, tiled=True)
    branch = jnp.dot(
        local_attn,
        lax.all_gather(w_proj, "seq", axis=0, tiled=True),
        preferred_element_type=jnp.float32,
    )
    outputs = [(source + branch).astype(jnp.bfloat16)]
    branches = [branch]
    block_out = jnp.stack(outputs)[None]
    branch_all = jnp.stack(branches)
    everything = lax.all_gather(branch_all[None], "section", axis=0, tiled=True)
    weights_all = jnp.sum(
        jnp.where(roles[:, None] == places[None, :], weight_table[None, :], 0.0), axis=1
    )
    gradient = jnp.tensordot(weights_all, everything, axes=1, precision=lax.Precision.HIGHEST)
    grad_bf = gradient.astype(jnp.bfloat16)
    column_width = width // lax.axis_size("section")
    first_column = section * column_width
    grad_columns = lax.dynamic_slice_in_dim(grad_bf, first_column, column_width, 2)
    inner_here = stored_attn.shape[2]
    local_grad = jnp.einsum(
        "bri,brc->ic",
        stored_attn,
        lax.all_gather(grad_columns, "seq", axis=1, tiled=True),
        preferred_element_type=jnp.float32,
    )
    placed = lax.dynamic_update_slice_in_dim(
        jnp.zeros((inner_here, width), jnp.float32), local_grad, first_column, 1
    )
    grad_out = lax.psum(placed, ("section", "dp"))
    return (block_out, gradient, grad_out)


def solution(mesh):
    placed = (
        P(),
        P(None, "dp", None),
        P("dp", "seq", None),
        P("dp", "seq", None),
        P("dp", None),
        P(None, None, "seq"),
        P(None, "seq", None),
        P("dp", None, "seq"),
    )
    return jax.shard_map(
        per_device,
        mesh=mesh,
        in_specs=placed,
        out_specs=(P("section", "dp", "seq", None), P("dp", "seq", None), P("seq", None)),
        check_vma=False,
    )
```

profile of v0, /device:TPU:2, one launch (start us, length us, event | category | flops | bytes accessed | tf_op | source)
XLA Modules:
  0.0 473.8 jit_solution(14698712417974718200)
XLA Ops:
  13.3 2.8 multiply_convert_fusion
  21.6 100.6 %all-gather.8.cloned.1.call-done = bf16[3072,2560]{1,0:T(8,128)(2,1)} async-done(((bf16[192,2560]{1,0:T(8,128)(2,1)}), bf16[3072,2560]{1,0:T(8,128)(2,1)}) %all-gather.8.cloned.1.call-update) | async-done | bytes 15728656 | tf_op jit(solution)/shard_map/all_gather | solution.py:75
  122.3 11.4 %convolution_convert_fusion = bf16[3072,384]{0,1:T(8,128)(2,1)} fusion(bf16[3072,2560]{1,0:T(8,128)(2,1)} %all-gather.8.cloned.1.call-done, bf16[3,2560,384]{2,1,0:T(8,128)(2,1)} %param.17, s32[]{:T(128)S(6)} %select_n.60), kind=kOutput, calls=%fused_computation.21 | convolution fusion | flops 6040977408 | bytes 20054020 | tf_op jit(solution)/shard_map/dot_general | solution.py:74
  133.6 3.1 copy.21
  138.0 46.5 %while.17 = (s32[]{:T(128)}, bf16[6,512,128]{2,1,0:T(8,128)(2,1)}, s32[3072]{0:T(1024)S(1)}, s32[6,512]{1,0:T(8,128)S(1)}, bf16[6,512,128]{2,1,0:T(8,128)(2,1)},...) while((s32[]{:T(128)}, bf16[6,512,128]{2,1,0:T(8,128)(2,1)}, s32[3072]{0:T(1024)S(1)}, ...), condition=%wide.region_6.7_spmd, body=%wide.region_3.6_spmd.sunk | while | flops 832109568 | bytes 20767832 | solution.py:45
  138.0 2.5 fusion.41
  142.6 3.1 fusion.43
  145.8 2.5 fusion.41
  150.4 3.1 fusion.43
  158.1 3.1 fusion.43
  161.3 2.5 fusion.41
  165.9 3.1 fusion.43
  173.6 3.1 fusion.43
  176.8 2.5 fusion.41
  181.4 3.1 fusion.43
  184.5 5.3 %all-to-all-start = ((bf16[16,192,128]{2,1,0:T(8,128)(2,1)}), bf16[16,192,128]{2,1,0:T(8,128)(2,1)S(1)}, u32[]{:S(2)}, u32[]{:S(2)}) async-start(bf16[16,192,128]{2,1,0:T(8,128)(2,1)} %bitcast.76), calls=%async_computation | async-start | bytes 1572864 | tf_op jit(solution)/shard_map/all_to_all | solution.py:79
  189.9 21.4 %all-gather.10.cloned.1.call-done = bf16[1,2048,2560]{2,1,0:T(8,128)(2,1)} async-done(((bf16[1,128,2560]{2,1,0:T(8,128)(2,1)}), bf16[1,2048,2560]{2,1,0:T(8,128)(2,1)}) %all-gather.10.cloned.1.call-update) | async-done | bytes 10485776 | tf_op jit(solution)/shard_map/all_gather | solution.py:82
  211.3 7.5 %fusion.13 = f32[192,2560]{1,0:T(8,128)} fusion(bf16[1,2048,2560]{2,1,0:T(8,128)(2,1)} %all-gather.10.cloned.1.call-done, bf16[16,192,128]{2,1,0:T(8,128)(2,1)S(1)} %all-to-all-done), kind=kOutput, calls=%fused_computation.17 | convolution fusion | flops 2013265920 | bytes 13238272 | tf_op jit(solution)/shard_map/dot_general | solution.py:80
  219.2 77.9 %all-gather.12.cloned.1.call-done = f32[768,2560]{1,0:T(8,128)} async-done(((f32[192,2560]{1,0:T(8,128)}), f32[768,2560]{1,0:T(8,128)}) %all-gather.12.cloned.1.call-update) | async-done | bytes 7864336 | tf_op jit(solution)/shard_map/all_gather | solution.py:89
  297.1 22.8 %fusion.15 = f32[1,192,2560]{2,0,1:T(1,128)S(1)} fusion(f32[4,192,2560]{2,1,0:T(8,128)} %bitcast.72, f32[4]{0:T(128)S(1)} %select_reduce_fusion), kind=kOutput, calls=%fused_computation.19 | convolution fusion | flops 23592960 | bytes 9830416 | tf_op jit(solution)/shard_map/dot_general | solution.py:93
  322.2 55.8 %all-gather.14.cloned.1.call-done = bf16[3072,640]{1,0:T(8,128)(2,1)} async-done(((bf16[192,640]{1,0:T(8,128)(2,1)}), bf16[3072,640]{1,0:T(8,128)(2,1)}) %all-gather.14.cloned.1.call-update) | async-done | bytes 3932176 | tf_op jit(solution)/shard_map/all_gather | solution.py:102
  378.0 3.3 convolution_bitcast_fusion
  383.5 3.3 fusion.20
  388.1 76.7 %all-reduce.2.cloned.1.call-done = f32[128,2560]{1,0:T(8,128)} async-done(((f32[128,2560]{1,0:T(8,128)}), f32[128,2560]{1,0:T(8,128)}) %all-reduce.2.cloned.1.call-update) | async-done | bytes 1310736 | tf_op jit(solution)/shard_map/psum | solution.py:108
  (64 shorter events, 35.1 us)
Async XLA Ops:
  7.2 12.3 %copy-start = (bf16[3,128,2560]{2,1,0:T(8,128)(2,1)S(1)}, bf16[3,128,2560]{2,1,0:T(8,128)(2,1)}, u32[]{:S(2)}) copy-start(bf16[3,128,2560]{2,1,0:T(8,128)(2,1)} %param.18) | copy-start | bytes 5898244
  7.2 9.0 %copy-start.9 = (s32[4]{0:T(128)S(1)}, s32[4]{0:T(128)}, u32[]{:S(2)}) copy-start(s32[4]{0:T(128)} %constant.69.clone) | copy-start | bytes 52
  7.2 13.7 %copy-start.6 = (s32[2,1,3072]{2,1,0:T(1,128)S(1)}, s32[2,1,3072]{2,1,0:T(1,128)}, u32[]{:S(2)}) copy-start(s32[2,1,3072]{2,1,0:T(1,128)} %param.13) | copy-start | bytes 73732
  7.2 115.1 %all-gather.8.cloned.1.call-start = ((), (), s32[]{:S(2)}) async-start(), calls=%async_computation.1 | async-start | bytes 16711680 | tf_op jit(solution)/shard_map/all_gather | solution.py:75
  16.2 195.1 %all-gather.10.cloned.1.call-start = ((), (), s32[]{:S(2)}) async-start(), calls=%async_computation.3 | async-start | bytes 11141120 | tf_op jit(solution)/shard_map/all_gather | solution.py:82
  184.5 26.8 %all-to-all-start = ((bf16[16,192,128]{2,1,0:T(8,128)(2,1)}), bf16[16,192,128]{2,1,0:T(8,128)(2,1)S(1)}, u32[]{:S(2)}, u32[]{:S(2)}) async-start(bf16[16,192,128]{2,1,0:T(8,128)(2,1)} %bitcast.76), calls=%async_computation | async-start | bytes 1572864 | tf_op jit(solution)/shard_map/all_to_all | solution.py:79
  189.8 29.2 %copy-start.7 = (s32[4]{0:T(128)S(1)}, s32[4]{0:T(128)}, u32[]{:S(2)}) copy-start(s32[4]{0:T(128)} %param.12) | copy-start | bytes 52
  189.8 29.2 %copy-start.8 = (f32[4]{0:T(128)S(1)}, f32[4]{0:T(128)}, u32[]{:S(2)}) copy-start(f32[4]{0:T(128)} %constant.68.clone) | copy-start | bytes 52
  189.9 107.3 %all-gather.12.cloned.1.call-start = ((), (), s32[]{:S(2)}) async-start(), calls=%async_computation.4 | async-start | bytes 9830400 | tf_op jit(solution)/shard_map/all_gather | solution.py:89
  218.8 159.2 %all-gather.14.cloned.1.call-start = ((), (), s32[]{:S(2)}) async-start(), calls=%async_computation.5 | async-start | bytes 4177920 | tf_op jit(solution)/shard_map/all_gather | solution.py:102
  297.1 80.8 %copy-start.5 = (bf16[1,3072,128]{2,1,0:T(8,128)(2,1)S(1)}, bf16[1,3072,128]{2,1,0:T(8,128)(2,1)}, u32[]{:S(2)}) copy-start(bf16[1,3072,128]{2,1,0:T(8,128)(2,1)} %param.19) | copy-start | bytes 2359300
  320.0 1.3 copy-start.2
  321.3 62.2 %copy-start.4 = (bf16[1,192,2560]{2,1,0:T(8,128)(2,1)S(1)}, bf16[1,192,2560]{2,1,0:T(8,128)(2,1)}, u32[]{:S(2)}) copy-start(bf16[1,192,2560]{2,1,0:T(8,128)(2,1)} %param.15) | copy-start | bytes 2949124
  322.2 142.7 %all-reduce.2.cloned.1.call-start = ((), (), s32[]{:S(2)}) async-start(), calls=%async_computation.2 | async-start | bytes 2621440 | tf_op jit(solution)/shard_map/psum | solution.py:108
  383.4 3.3 copy-start.3
  383.4 83.9 %copy-start.1 = (bf16[3,128,2560]{2,1,0:T(8,128)(2,1)S(1)}, bf16[3,128,2560]{2,1,0:T(8,128)(2,1)}, u32[]{:S(2)}) copy-start(bf16[3,128,2560]{2,1,0:T(8,128)(2,1)} %param.18) | copy-start | bytes 5898244
Sparse Core Ops, SparseCore 0:
  16.3 105.9 all-gather.7
  124.7 86.5 all-gather.9
  218.9 78.1 all-gather.11
  322.3 55.6 all-gather.13
  383.5 81.2 all-reduce.1
where the time goes:
time: 475 us; the launch traced here: 474 us
  waiting for transfers between devices  332 us (70%)
  matrix products  79 us (17%)
  other arithmetic  24.8 us (5%)
  between operations  17.8 us (4%)
  local copies, waits for them, and re-layouts  14 us (3%)
  starting transfers between devices  5.73 us (1%)
    all_gather x1, waiting for transfers between devices, per_device(): lax.all_gather(normed, 'seq', axis=0, tiled=True)  101 us
    all_gather x1, waiting for transfers between devices, per_device(): everything = lax.all_gather(branch_all[None], 'section', axis=0, tiled=True)  77.9 us
    psum x1, waiting for transfers between devices, per_device(): grad_out = lax.psum(placed, ('section', 'dp'))  76.7 us
    all_gather x1, waiting for transfers between devices, per_device(): lax.all_gather(grad_columns, 'seq', axis=1, tiled=True)  55.8 us
    dot_general x1, matrix products, per_device(): jnp.tensordot(weights_all, everything, axes=1, precision=lax.Precision.HI...  22.8 us
    all_gather x1, waiting for transfers between devices, per_device(): lax.all_gather(w_proj, 'seq', axis=0, tiled=True)  21.4 us
    dot_general x6, matrix products, per_block(): jnp.dot(probs, values, preferred_element_type=jnp.float32)  18.9 us
    dot_general x6, matrix products, per_block(): lax.dot_general(query_rows, keys_all, (((1,), (1,)), ((), ())), preferred...  15.1 us
  transfers between devices with their start and end apart: 6, of which 5 were waited for; matrix products, arithmetic and copies ran while one was open for 15% of the time, Pallas kernels for 0%

commit v1 on v0

v1 whole, which is shorter than its diff:
```python
import jax
import jax.numpy as jnp
import numpy as np
from jax import lax
from jax.experimental import pallas as pl
from jax.experimental.pallas import tpu as pltpu
from jax.sharding import Mesh
from jax.sharding import PartitionSpec as P

HEAD_DIM = 128
GUIDE = 3.0
EPSILON = 1e-06
NEGATIVE = -1e30
QUERY_TILE = 512
KEY_TILE = 512
LOG2E = 1.4426950408889634
RING = ("x", "zhi")
SEQ = ("x", "zhi", "core")


def attention_kernel(bounds, qkv, seen, out, values, top, acc):
    tile = pl.program_id(0)
    length = qkv.shape[0]

    @pl.when(tile == 0)
    def _():
        values[:, :HEAD_DIM] = qkv[:, 2 * HEAD_DIM :]
        values[:, HEAD_DIM:] = jnp.ones((length, HEAD_DIM), jnp.bfloat16)

    start = pl.multiple_of(tile * QUERY_TILE, QUERY_TILE)
    queries = qkv[pl.ds(start, QUERY_TILE), :HEAD_DIM]
    factor = LOG2E * HEAD_DIM ** (-0.5)
    top[...] = jnp.full(top.shape, NEGATIVE, jnp.float32)
    acc[...] = jnp.zeros(acc.shape, jnp.float32)

    def step(j, masked):
        first = pl.multiple_of(j * KEY_TILE, KEY_TILE)
        keys = qkv[pl.ds(first, KEY_TILE), HEAD_DIM : 2 * HEAD_DIM]
        scores = lax.dot_general(
            queries, keys, (((1,), (1,)), ((), ())), preferred_element_type=jnp.float32
        ) * factor
        if masked:
            place = lax.broadcasted_iota(jnp.int32, scores.shape, 1) + first
            scores = jnp.where(place < seen[...], scores, NEGATIVE)
        old = top[...]
        new = jnp.maximum(old, jnp.max(scores, axis=1, keepdims=True))
        top[...] = new
        weights = jnp.exp2(scores - new).astype(jnp.bfloat16)
        acc[...] = acc[...] * jnp.exp2(old - new) + jnp.dot(
            weights, values[pl.ds(first, KEY_TILE), :], preferred_element_type=jnp.float32
        )

    whole = bounds[tile, 0]

    @pl.loop(0, whole)
    def _(j):
        step(j, False)

    @pl.loop(whole, bounds[tile, 1])
    def _(j):
        step(j, True)

    out[...] = (acc[:, :HEAD_DIM] / acc[:, HEAD_DIM:]).astype(jnp.bfloat16)


def attend(qkv_rows, frame_ids):
    length = qkv_rows.shape[0]
    tiles = length // QUERY_TILE
    seen = jnp.sum((frame_ids[None, :] <= frame_ids[:, None]).astype(jnp.int32), axis=1)
    per_tile = seen.reshape(tiles, QUERY_TILE)
    bounds = jnp.stack(
        [per_tile[:, 0] // KEY_TILE, (per_tile[:, -1] + KEY_TILE - 1) // KEY_TILE], axis=1
    )
    return pl.pallas_call(
        attention_kernel,
        out_shape=jax.ShapeDtypeStruct((length, HEAD_DIM), jnp.bfloat16),
        grid_spec=pltpu.PrefetchScalarGridSpec(
            num_scalar_prefetch=1,
            grid=(tiles,),
            in_specs=[
                pl.BlockSpec((length, 3 * HEAD_DIM), lambda i, b: (0, 0)),
                pl.BlockSpec((QUERY_TILE, 1), lambda i, b: (i, 0)),
            ],
            out_specs=pl.BlockSpec((QUERY_TILE, HEAD_DIM), lambda i, b: (i, 0)),
            scratch_shapes=[
                pltpu.VMEM((length, 2 * HEAD_DIM), jnp.bfloat16),
                pltpu.VMEM((QUERY_TILE, 1), jnp.float32),
                pltpu.VMEM((QUERY_TILE, 2 * HEAD_DIM), jnp.float32),
            ],
        ),
        name="attend",
    )(bounds, qkv_rows, seen[:, None])


def per_device(roles, block_ids, latent, pending, context, w_qkv, w_out, stored_attn):
    section = lax.axis_index("section")
    places = jnp.arange(4, dtype=jnp.int32)
    weight_table = jnp.array([0.0, -GUIDE, GUIDE - 1.0, 1.0], jnp.float32)
    section_role = jnp.sum(jnp.where(places == section, roles, 0))
    model_index = jnp.sum(jnp.where(places == section_role, jnp.array([0, 1, 1, 2], jnp.int32), 0))
    own_weight = jnp.sum(jnp.where(places == section_role, weight_table, 0.0))
    w_in = lax.dynamic_index_in_dim(w_qkv, model_index, 0, keepdims=False)
    w_proj = lax.dynamic_index_in_dim(w_out, model_index, 0, keepdims=False)
    is_generator = section_role == 0
    with_context = jnp.logical_or(section_role == 1, section_role == 3).astype(jnp.float32)
    rows, width = latent.shape[1:]
    scored = pending[0].astype(jnp.float32) + with_context * context[0][None, :]
    source = jnp.where(is_generator, latent[0].astype(jnp.float32), scored)
    normed = (
        source * lax.rsqrt(jnp.mean(source * source, axis=1, keepdims=True) + EPSILON)
    ).astype(jnp.bfloat16)
    qkv_rows = jnp.dot(
        lax.all_gather(normed, SEQ, axis=0, tiled=True), w_in, preferred_element_type=jnp.float32
    ).astype(jnp.bfloat16)
    frame_ids = jnp.where(is_generator, block_ids[0, 0], block_ids[1, 0])
    attn = attend(qkv_rows, frame_ids)
    local_attn = lax.all_to_all(attn, SEQ, split_axis=0, concat_axis=1, tiled=True)
    branch = jnp.dot(
        local_attn,
        lax.all_gather(w_proj, SEQ, axis=0, tiled=True),
        preferred_element_type=jnp.float32,
    )
    block_out = (source + branch).astype(jnp.bfloat16)[None, None]
    return (block_out,) + gradients(own_weight, branch, stored_attn)


def gradients(own_weight, branch, stored_attn):
    rows, width = branch.shape
    sections = lax.axis_size("section")
    part = width // sections
    terms = (own_weight * branch).astype(jnp.bfloat16)
    terms = terms.reshape(rows, sections, part).transpose(1, 0, 2)
    terms = lax.all_to_all(terms, "section", 0, 0, tiled=True)
    grad_bf = jnp.sum(terms.astype(jnp.float32), axis=0).astype(jnp.bfloat16)
    gradient = lax.all_gather(grad_bf, "section", axis=1, tiled=True).astype(jnp.float32)[None]
    core = lax.axis_index("core")
    other = lax.ppermute(grad_bf, "core", [(0, 1), (1, 0)])
    both = jnp.where(core == 0, jnp.stack([grad_bf, other]), jnp.stack([other, grad_bf]))
    both = both.reshape(2 * rows, part)
    chips = lax.axis_size("x") * lax.axis_size("zhi")
    inner_here = stored_attn.shape[2]
    stored = lax.all_to_all(
        stored_attn.reshape(chips, 2 * rows, inner_here), RING, 0, 0, tiled=True
    )
    product = jnp.einsum("hri,rc->hic", stored, both, preferred_element_type=jnp.float32)
    product = product.astype(jnp.bfloat16).reshape(chips, inner_here, 2, part // 2)
    product = product.transpose(0, 2, 1, 3).reshape(chips * 2, inner_here, part // 2)
    product = lax.all_to_all(product, RING + ("dp",), 0, 0, tiled=True)
    total = jnp.sum(product.astype(jnp.float32), axis=0).astype(jnp.bfloat16)
    grad_out = lax.all_gather(total, ("section", "dp"), axis=1, tiled=True).astype(jnp.float32)
    return (gradient, grad_out)


def solution(mesh):
    fine = Mesh(mesh.devices.reshape(4, 4, 2, 2, 2), ("section", "x", "zhi", "core", "dp"))
    placed = (
        P(),
        P(None, "dp", None),
        P("dp", SEQ, None),
        P("dp", SEQ, None),
        P("dp", None),
        P(None, None, SEQ),
        P(None, SEQ, None),
        P("dp", None, SEQ),
    )
    return jax.shard_map(
        per_device,
        mesh=fine,
        in_specs=placed,
        out_specs=(P("section", "dp", SEQ, None), P("dp", SEQ, None), P(SEQ, None)),
        check_vma=False,
    )
```

time: 475 us -> 327 us (0.69)
  waiting for transfers between devices: 332 us -> 143 us
  blocking collectives: 0 us -> 63.7 us
  matrix products: 79 us -> 23.6 us
  Pallas kernels: 0 us -> 34.6 us
  starting transfers between devices: 5.73 us -> 17 us
  other arithmetic: 24.8 us -> 14.8 us
  local copies, waits for them, and re-layouts: 14 us -> 8.81 us
    all_gather x4 -> x2, waiting for transfers between devices: 256 us -> 131 us  [the longest x1 95.7 us: per_device(): lax.all_gather(normed, SEQ, axis=0, tiled=True)]
    psum x1 -> x0, waiting for transfers between devices: 76.7 us -> none  [per_device(): grad_out = lax.psum(placed, ('section', 'dp'))]
    dot_general x16 -> x3, matrix products: 79 us -> 23.6 us  [the longest x1 13.3 us: per_device(): jnp.dot(lax.all_gather(normed, SEQ, axis=0, tiled=True), w_in, preferred_...]
    all_gather x0 -> x2, blocking collectives: none -> 44.8 us  [the longest x1 29.3 us: gradients(): lax.all_gather(total, ('section', 'dp'), axis=1, tiled=True)]
    pallas_call x0 -> x1, Pallas kernels: none -> 34.6 us  [attend(): pl.pallas_call(attention_kernel, out_shape=jax.ShapeDtypeStruct((length,...]
    all_to_all x0 -> x1, blocking collectives: none -> 18.9 us  [gradients(): terms = lax.all_to_all(terms, 'section', 0, 0, tiled=True)]
    all_to_all x1 -> x3, starting transfers between devices: 5.34 us -> 16.8 us  [the longest x1 5.96 us: per_device(): lax.all_to_all(attn, SEQ, split_axis=0, concat_axis=1, tiled=True)]
    all_to_all x1 -> x3, waiting for transfers between devices: 0.01 us -> 10.6 us  [the longest x1 9.98 us: gradients(): lax.all_to_all(stored_attn.reshape(chips, 2 * rows, inner_here), RING, 0,...]
  transfers between devices with their start and end apart: 6 -> 6, of which waited for: 5 -> 5; matrix products, arithmetic and copies ran while one was open for 15% -> 8% of each run, Pallas kernels for 0% -> 11%
where the time goes in v1:
time: 327 us; the launch traced here: 323 us
  waiting for transfers between devices  143 us (44%)
  blocking collectives  63.7 us (19%)
  Pallas kernels  34.6 us (11%)
  matrix products  23.6 us (7%)
  between operations  18 us (6%)
  starting transfers between devices  17 us (5%)
  other arithmetic  14.8 us (5%)
  local copies, waits for them, and re-layouts  8.81 us (3%)
    all_gather x1, waiting for transfers between devices, per_device(): lax.all_gather(normed, SEQ, axis=0, tiled=True)  95.7 us
    all_gather x1, waiting for transfers between devices, per_device(): lax.all_gather(w_proj, SEQ, axis=0, tiled=True)  35.2 us
    pallas_call x1, Pallas kernels, attend(): pl.pallas_call(attention_kernel, out_shape=jax.ShapeDtypeStruct((length,...  34.6 us
    all_gather x1, blocking collectives, gradients(): lax.all_gather(total, ('section', 'dp'), axis=1, tiled=True)  29.3 us
    all_to_all x1, blocking collectives, gradients(): terms = lax.all_to_all(terms, 'section', 0, 0, tiled=True)  18.9 us
    all_gather x1, blocking collectives, gradients(): lax.all_gather(grad_bf, 'section', axis=1, tiled=True).astype(jnp.float32)  15.5 us
    dot_general x1, matrix products, per_device(): jnp.dot(lax.all_gather(normed, SEQ, axis=0, tiled=True), w_in, preferred_...  13.3 us
    all_to_all x1, waiting for transfers between devices, gradients(): lax.all_to_all(stored_attn.reshape(chips, 2 * rows, inner_here), RING, 0,...  9.98 us
  transfers between devices with their start and end apart: 6, of which 5 were waited for; matrix products, arithmetic and copies ran while one was open for 8% of the time, Pallas kernels for 11%

profile of v1, /device:TPU:2, one launch (start us, length us, event | category | flops | bytes accessed | tf_op | source)
XLA Modules:
  0.0 323.4 jit_solution(488745657015072242)
XLA Ops:
  7.2 1.5 fusion.15
  11.5 2.0 multiply_reduce_fusion
  13.5 1.3 multiply_convert_fusion.1
  14.9 1.2 fusion.13
  19.0 3.8 %convert_reduce_fusion = s32[3072]{0:T(1024)S(1)} fusion(s32[3072]{0:T(1024)S(1)} %bitcast.64), kind=kLoop, calls=%fused_computation | loop fusion | flops 28308480 | bytes 24576 | tf_op jit(solution)/shard_map/reduce_sum | solution.py:69
  22.8 1.7 copy.38.seen
  25.2 95.7 %all-gather.4.cloned.1.call-done = bf16[3072,2560]{1,0:T(8,128)(2,1)} async-done(((bf16[192,2560]{1,0:T(8,128)(2,1)}), bf16[3072,2560]{1,0:T(8,128)(2,1)}) %all-gather.4.cloned.1.call-update) | async-done | bytes 15728656 | tf_op jit(solution)/shard_map/all_gather | solution.py:113
  120.9 13.3 %convolution_convert_fusion.qkv = bf16[3072,384]{1,0:T(8,128)(2,1)} fusion(bf16[3072,2560]{1,0:T(8,128)(2,1)} %all-gather.4.cloned.1.call-done, bf16[3,2560,384]{2,1,0:T(8,128)(2,1)} %param.15, s32[]{:T(128)S(6)} %select_n.76), kind=kOutput, calls=%fused_computation.3 | convolution fusion | flops 6040977408 | bytes 20054020 | tf_op jit(solution)/shard_map/dot_general | solution.py:112
  134.2 34.6 %attend.1 = bf16[3072,128]{1,0:T(8,128)(2,1)} custom-call(s32[6,2]{1,0:T(8,128)} %pad_add_fusion.bounds, bf16[3072,384]{1,0:T(8,128)(2,1)} %convolution_convert_fusion.qkv, s32[3072,1]{1,0:T(8,128)} %copy.38.seen), custom_call_target="tpu_custom_call" | custom-call | tf_op jit(solution)/shard_map/attend/pallas_call | solution.py:74
  168.8 6.0 %all-to-all-start = ((bf16[16,192,128]{2,1,0:T(8,128)(2,1)}), bf16[16,192,128]{2,1,0:T(8,128)(2,1)}, u32[]{:S(2)}, u32[]{:S(2)}) async-start(bf16[16,192,128]{2,1,0:T(8,128)(2,1)} %bitcast.57), calls=%async_computation | async-start | bytes 1572864 | tf_op jit(solution)/shard_map/all_to_all | solution.py:117
  176.0 35.2 %all-gather.6.cloned.1.call-done = bf16[1,2048,2560]{2,1,0:T(8,128)(2,1)} async-done(((bf16[1,128,2560]{2,1,0:T(8,128)(2,1)}), bf16[1,2048,2560]{2,1,0:T(8,128)(2,1)}) %all-gather.6.cloned.1.call-update) | async-done | bytes 10485776 | tf_op jit(solution)/shard_map/all_gather | solution.py:120
  211.2 8.2 %multiply_convert_fusion = (bf16[192,2560]{1,0:T(8,128)(2,1)S(1)}, bf16[1,1,192,2560]{3,2,1,0:T(8,128)(2,1)}) fusion(f32[]{:T(128)} %fusion.14, f32[2560]{0:T(1024)S(1)} %multiply_reduce_fusion.1, bf16[1,192,2560]{2,1,0:T(8,128)(2,1)S(1)} %copy-done.1, bf16[1,192,2560]{2,1,0:T(8,128)(2,1)} %param.12, pred[]{:T(512)S(6)} %eq.28, ...), kind=kOutput, calls=%fused_computation.7 | convolution fusion | flops 2017198080 | bytes 15214597 | tf_op jit(solution)/shard_map/dot_general | solution.py:118
  219.5 18.9 %all_to_all.34 = bf16[4,192,640]{2,1,0:T(8,128)(2,1)S(1)} all-to-all(bf16[4,192,640]{2,1,0:T(8,128)(2,1)S(1)} %bitcast.56), channel_id=1, replica_groups=mesh['section'=4,'x'=4,'zhi'=2,'core'=2,'dp'=2] {'section'}, dimensions={0} | all-to-all | bytes 1966080 | tf_op jit(solution)/shard_map/all_to_all | solution.py:133
  238.4 5.9 %all-to-all-start.2 = ((bf16[8,384,128]{2,1,0:T(8,128)(2,1)}), bf16[8,384,128]{2,1,0:T(8,128)(2,1)}, u32[]{:S(2)}, u32[]{:S(2)}) async-start(bf16[8,384,128]{2,1,0:T(8,128)(2,1)} %bitcast.60), calls=%async_computation.2 | async-start | bytes 1572864 | tf_op jit(solution)/shard_map/all_to_all | solution.py:142
  244.6 1.5 collective-permute-done
  246.2 10.0 %all-to-all-done.2 = bf16[8,384,128]{2,1,0:T(8,128)(2,1)} async-done(((bf16[8,384,128]{2,1,0:T(8,128)(2,1)}), bf16[8,384,128]{2,1,0:T(8,128)(2,1)}, u32[]{:S(2)}, u32[]{:S(2)}) %all-to-all-start.2) | async-done | bytes 786464 | tf_op jit(solution)/shard_map/all_to_all | solution.py:142
  256.2 2.0 fusion.5
  259.2 1.3 reshape.62
  260.5 2.7 copy.43
  263.2 4.9 %all-to-all-start.3 = ((bf16[16,128,320]{1,2,0:T(8,128)(2,1)}), bf16[16,128,320]{1,2,0:T(8,128)(2,1)S(1)}, u32[]{:S(2)}, u32[]{:S(2)}) async-start(bf16[16,128,320]{1,2,0:T(8,128)(2,1)} %copy.43), calls=%async_computation.3 | async-start | bytes 2621440 | tf_op jit(solution)/shard_map/all_to_all | solution.py:148
  268.1 15.5 %all_gather.14 = bf16[192,2560]{1,0:T(8,128)(2,1)S(1)} all-gather(bf16[192,640]{1,0:T(8,128)(2,1)S(1)} %reduce_sum.74), channel_id=1, replica_groups=mesh['section'=4,'x'=4,'zhi'=2,'core'=2,'dp'=2] {'section'}, dimensions={1}, use_global_device_ids=true | all-gather | bytes 1228800 | tf_op jit(solution)/shard_map/all_gather | solution.py:135
  283.6 1.5 bitcast_convert_fusion
  285.9 29.3 %all_gather.15 = bf16[128,2560]{0,1:T(8,128)(2,1)S(1)} all-gather(bf16[128,320]{0,1:T(8,128)(2,1)S(1)} %reduce_sum.75), channel_id=1, replica_groups=mesh['section'=4,'x'=4,'zhi'=2,'core'=2,'dp'=2] {'section','dp'}, dimensions={1}, use_global_device_ids=true | all-gather | bytes 737280 | tf_op jit(solution)/shard_map/all_gather | solution.py:150
  315.2 1.3 copy.45
  (34 shorter events, 6.1 us)
Async XLA Ops:
  7.2 10.9 %copy-start = (bf16[3,128,2560]{2,1,0:T(8,128)(2,1)S(1)}, bf16[3,128,2560]{2,1,0:T(8,128)(2,1)}, u32[]{:S(2)}) copy-start(bf16[3,128,2560]{2,1,0:T(8,128)(2,1)} %param.16) | copy-start | bytes 5898244
  7.2 6.3 %copy-start.1 = (bf16[1,192,2560]{2,1,0:T(8,128)(2,1)S(1)}, bf16[1,192,2560]{2,1,0:T(8,128)(2,1)}, u32[]{:S(2)}) copy-start(bf16[1,192,2560]{2,1,0:T(8,128)(2,1)} %param.13) | copy-start | bytes 2949124
  7.2 113.7 %all-gather.4.cloned.1.call-start = ((), (), s32[]{:S(2)}) async-start(), calls=%async_computation.4 | async-start | bytes 16711680 | tf_op jit(solution)/shard_map/all_gather | solution.py:113
  10.6 2.8 copy-start.2
  13.5 1.4 copy-start.5
  14.8 4.2 %copy-start.3 = (s32[2,1,3072]{2,1,0:T(1,128)S(1)}, s32[2,1,3072]{2,1,0:T(1,128)}, u32[]{:S(2)}) copy-start(s32[2,1,3072]{2,1,0:T(1,128)} %param.11) | copy-start | bytes 73732
  14.8 196.4 %all-gather.6.cloned.1.call-start = ((), (), s32[]{:S(2)}) async-start(), calls=%async_computation.5 | async-start | bytes 11141120 | tf_op jit(solution)/shard_map/all_gather | solution.py:120
  134.2 40.5 %copy-start.4 = (f32[4]{0:T(128)S(1)}, f32[4]{0:T(128)}, u32[]{:S(2)}) copy-start(f32[4]{0:T(128)} %constant.63.clone) | copy-start | bytes 52
  168.8 42.4 %all-to-all-start = ((bf16[16,192,128]{2,1,0:T(8,128)(2,1)}), bf16[16,192,128]{2,1,0:T(8,128)(2,1)}, u32[]{:S(2)}, u32[]{:S(2)}) async-start(bf16[16,192,128]{2,1,0:T(8,128)(2,1)} %bitcast.57), calls=%async_computation | async-start | bytes 1572864 | tf_op jit(solution)/shard_map/all_to_all | solution.py:117
  238.4 17.8 %all-to-all-start.2 = ((bf16[8,384,128]{2,1,0:T(8,128)(2,1)}), bf16[8,384,128]{2,1,0:T(8,128)(2,1)}, u32[]{:S(2)}, u32[]{:S(2)}) async-start(bf16[8,384,128]{2,1,0:T(8,128)(2,1)} %bitcast.60), calls=%async_computation.2 | async-start | bytes 1572864 | tf_op jit(solution)/shard_map/all_to_all | solution.py:142
  244.5 1.6 collective-permute-start
  263.2 22.5 %all-to-all-start.3 = ((bf16[16,128,320]{1,2,0:T(8,128)(2,1)}), bf16[16,128,320]{1,2,0:T(8,128)(2,1)S(1)}, u32[]{:S(2)}, u32[]{:S(2)}) async-start(bf16[16,128,320]{1,2,0:T(8,128)(2,1)} %copy.43), calls=%async_computation.3 | async-start | bytes 2621440 | tf_op jit(solution)/shard_map/all_to_all | solution.py:148
Sparse Core Ops, SparseCore 0:
  14.9 105.9 all-gather.3
  123.9 87.2 all-gather.5

commit v2 on v1

v2 whole, which is shorter than its diff:
```python
import jax
import jax.numpy as jnp
from jax import lax
from jax.experimental import pallas as pl
from jax.experimental.pallas import tpu as pltpu
from jax.sharding import Mesh
from jax.sharding import PartitionSpec as P


HEAD_DIM = 128
GUIDE = 3.0
EPSILON = 1e-06
NEGATIVE = -1e30
QUERY_TILE = 512
QUERY_PART = 256
KEY_TILE = 512
SCORE_SCALE = 1.4426950408889634 * HEAD_DIM ** (-0.5)
RING = ("x", "zhi")
SEQ = ("x", "zhi", "core")
SWAP = [(0, 1), (1, 0)]


def attention_kernel(bounds, starts, *refs):
    pieces = refs[:8]
    seen, out, qkv, values, top, acc, sems = refs[8:]
    tile = pl.program_id(0)
    length = qkv.shape[0]
    chips = 8
    chunk = pieces[0].shape[0] // chips

    @pl.when(tile == 0)
    def _():
        copies = []
        for i, piece in enumerate(pieces):
            for b in range(chips):
                place = pl.multiple_of(starts[i] * chunk + b * (length // chips), chunk)
                copies.append(
                    pltpu.make_async_copy(
                        piece.at[pl.ds(b * chunk, chunk)],
                        qkv.at[pl.ds(place, chunk)],
                        sems.at[i, b],
                    )
                )
        for copy in copies:
            copy.start()
        for copy in copies:
            copy.wait()
        values[:, :HEAD_DIM] = qkv[:, 2 * HEAD_DIM :]
        values[:, HEAD_DIM:] = jnp.ones((length, HEAD_DIM), jnp.bfloat16)

    top[...] = jnp.full(top.shape, NEGATIVE, jnp.float32)
    acc[...] = jnp.zeros(acc.shape, jnp.float32)
    parts = QUERY_TILE // QUERY_PART

    def step(j, masked):
        first = pl.multiple_of(j * KEY_TILE, KEY_TILE)
        keys = qkv[pl.ds(first, KEY_TILE), HEAD_DIM : 2 * HEAD_DIM]
        value = values[pl.ds(first, KEY_TILE), :]
        scores = []
        for i in range(parts):
            start = pl.multiple_of(tile * QUERY_TILE + i * QUERY_PART, QUERY_PART)
            score = lax.dot_general(
                qkv[pl.ds(start, QUERY_PART), :HEAD_DIM],
                keys,
                (((1,), (1,)), ((), ())),
                preferred_element_type=jnp.float32,
            )
            if masked:
                place = lax.broadcasted_iota(jnp.int32, score.shape, 1) + first
                limit = seen[pl.ds(i * QUERY_PART, QUERY_PART), :]
                score = jnp.where(place < limit, score, NEGATIVE)
            scores.append(score)
        olds = [top[i] for i in range(parts)]
        news = [
            jnp.maximum(old, jnp.max(score, axis=1, keepdims=True))
            for old, score in zip(olds, scores)
        ]
        for i in range(parts):
            weights = jnp.exp2(scores[i] - news[i]).astype(jnp.bfloat16)
            acc[i] = acc[i] * jnp.exp2(olds[i] - news[i]) + jnp.dot(
                weights, value, preferred_element_type=jnp.float32
            )
            top[i] = news[i]

    whole = bounds[tile, 0]

    @pl.loop(0, whole)
    def _(j):
        step(j, False)

    @pl.loop(whole, bounds[tile, 1])
    def _(j):
        step(j, True)

    for i in range(parts):
        out[pl.ds(i * QUERY_PART, QUERY_PART), :] = (
            acc[i, :, :HEAD_DIM] / acc[i, :, HEAD_DIM:]
        ).astype(jnp.bfloat16)


def visibility(frame_ids):
    length = frame_ids.shape[0]
    tiles = length // QUERY_TILE
    seen = jnp.sum((frame_ids[None, :] <= frame_ids[:, None]).astype(jnp.int32), axis=1)
    per_tile = seen.reshape(tiles, QUERY_TILE)
    bounds = jnp.stack(
        [per_tile[:, 0] // KEY_TILE, (per_tile[:, -1] + KEY_TILE - 1) // KEY_TILE], axis=1
    )
    return seen[:, None], bounds


def attend(pieces, starts, seen, bounds):
    length = seen.shape[0]
    wide = pieces[0].shape[1]
    parts = QUERY_TILE // QUERY_PART
    return pl.pallas_call(
        attention_kernel,
        out_shape=jax.ShapeDtypeStruct((length, HEAD_DIM), jnp.bfloat16),
        grid_spec=pltpu.PrefetchScalarGridSpec(
            num_scalar_prefetch=2,
            grid=(length // QUERY_TILE,),
            in_specs=[pl.BlockSpec(memory_space=pl.ANY)] * 8
            + [pl.BlockSpec((QUERY_TILE, 1), lambda i, b, s: (i, 0))],
            out_specs=pl.BlockSpec((QUERY_TILE, HEAD_DIM), lambda i, b, s: (i, 0)),
            scratch_shapes=[
                pltpu.VMEM((length, wide), jnp.bfloat16),
                pltpu.VMEM((length, 2 * HEAD_DIM), jnp.bfloat16),
                pltpu.VMEM((parts, QUERY_PART, 1), jnp.float32),
                pltpu.VMEM((parts, QUERY_PART, 2 * HEAD_DIM), jnp.float32),
                pltpu.SemaphoreType.DMA((8, 8)),
            ],
        ),
        name="attend",
    )(bounds, starts, *pieces, seen)


def project_kernel(place, *refs):
    rows = refs[:10]
    context, w_mine, w_other = refs[10:13]
    outs, (sources, scales) = refs[13:21], refs[21:]
    step = pl.program_id(0)
    chunk = rows[0].shape[1]

    @pl.when(step == 0)
    def _():
        added = context[...]
        for side in range(2):
            own, right, far_scored, far_latent, left = rows[side * 5 : side * 5 + 5]
            found = [(own[0], own[1]), (right[0], right[1])]
            found += [(far_scored[...], far_latent[...]), (left[0], left[1])]
            for i, (scored, latent) in enumerate(found):
                at = pl.ds(pl.multiple_of(place[4 + side * 4 + i] * chunk, chunk), chunk)
                wide = scored.astype(jnp.float32)
                shifted = wide + added
                sources[0, at, :] = scored
                sources[1, at, :] = shifted.astype(jnp.bfloat16)
                sources[2, at, :] = latent
                for j, v in enumerate((wide, shifted, latent.astype(jnp.float32))):
                    scales[j, at, :] = lax.rsqrt(
                        jnp.mean(v * v, axis=1, keepdims=True) + EPSILON
                    )

    role = place[step]
    kind = jnp.where(role == 0, 2, role % 2)
    left = sources[kind]
    scale = scales[kind]
    made = [
        jnp.dot(left, weights[0], preferred_element_type=jnp.float32) * scale
        for weights in (w_mine, w_other)
    ]
    for i in range(4):

        @pl.when(step == i)
        def _():
            for side in range(2):
                out = outs[2 * i + side]
                out[:, :HEAD_DIM] = (made[side][:, :HEAD_DIM] * SCORE_SCALE).astype(jnp.bfloat16)
                out[:, HEAD_DIM:] = made[side][:, HEAD_DIM:].astype(jnp.bfloat16)


def project(place, rows, context, w_mine, w_other):
    chunk, width = rows[0].shape[1:]
    many = 8 * chunk
    columns = w_mine.shape[2]
    picked = pl.BlockSpec((1, width, columns), lambda t, r: ((r[t] + 1) // 2, 0, 0))
    whole = pl.BlockSpec(memory_space=pltpu.VMEM)
    return pl.pallas_call(
        project_kernel,
        out_shape=[jax.ShapeDtypeStruct((many, columns), jnp.bfloat16)] * 8,
        grid_spec=pltpu.PrefetchScalarGridSpec(
            num_scalar_prefetch=1,
            grid=(4,),
            in_specs=[whole] * 11 + [picked, picked],
            out_specs=[pl.BlockSpec((many, columns), lambda t, r: (0, 0))] * 8,
            scratch_shapes=[
                pltpu.VMEM((3, many, width), jnp.bfloat16),
                pltpu.VMEM((3, many, 1), jnp.float32),
            ],
        ),
        name="project",
    )(place, *rows, context, w_mine, w_other)


def place_kernel(starts, *refs):
    out = refs[-1]
    for i, piece in enumerate(refs[:-1]):
        rows, columns = piece.shape
        row = pl.multiple_of(starts[i, 0], rows)
        column = pl.multiple_of(starts[i, 1], columns)
        out[pl.ds(row, rows), pl.ds(column, columns)] = piece[...].astype(jnp.float32)


def place_all(starts, pieces, shape):
    vmem = pl.BlockSpec(memory_space=pltpu.VMEM)
    return pl.pallas_call(
        place_kernel,
        out_shape=jax.ShapeDtypeStruct(shape, jnp.float32),
        in_specs=[pl.BlockSpec(memory_space=pltpu.SMEM)] + [vmem] * len(pieces),
        out_specs=vmem,
        name="place_all",
    )(starts, *pieces)


def moved(axis, size, step):
    return [(i, (i + step) % size) for i in range(size)]


def moved(axis, size, step):
    return [(i, (i + step) % size) for i in range(size)]


def per_device(roles, block_ids, latent, pending, context, w_qkv, w_out, stored_attn):
    section, core = lax.axis_index("section"), lax.axis_index("core")
    section_role = lax.dynamic_index_in_dim(roles, section, 0, keepdims=False)
    own_weight = jnp.where(
        section_role == 1,
        -GUIDE,
        jnp.where(section_role == 2, GUIDE - 1.0, jnp.where(section_role == 3, 1.0, 0.0)),
    )
    is_generator = section_role == 0
    with_context = (section_role % 2).astype(jnp.float32)
    rows, _ = latent.shape[1:]
    chunk = rows // lax.axis_size("section")

    quarter = jnp.stack(
        [
            lax.dynamic_slice_in_dim(pending[0], section * chunk, chunk, 0),
            lax.dynamic_slice_in_dim(latent[0], section * chunk, chunk, 0),
        ]
    )
    w_proj = lax.dynamic_index_in_dim(w_out, (section_role + 1) // 2, 0, keepdims=False)
    inner = w_proj.shape[0]
    w_wide = jnp.broadcast_to(w_proj[None], (8,) + w_proj.shape)
    frame_ids = jnp.where(is_generator, block_ids[0, 0], block_ids[1, 0])
    seen, bounds = visibility(frame_ids)

    theirs = lax.ppermute(quarter, "zhi", SWAP)
    everything = []
    for ours in (quarter, theirs):
        left = lax.ppermute(ours, "x", moved("x", 4, 1))
        right = lax.ppermute(ours, "x", moved("x", 4, -1))
        far_scored = lax.ppermute(left[0], "x", moved("x", 4, 1))
        far_latent = lax.ppermute(right[1], "x", moved("x", 4, -1))
        everything += [ours, right, far_scored, far_latent, left]
    everything, w_wide = lax.optimization_barrier((everything, w_wide))
    w_other = lax.ppermute(w_qkv, "core", SWAP)
    ahead = jnp.arange(4, dtype=jnp.int32)
    near = (lax.axis_index("x") + ahead) % 4 * 2
    zhi = lax.axis_index("zhi")
    place = jnp.concatenate(
        [jnp.roll(roles, -section), near + zhi, near + (1 - zhi)]
    )
    made = project(place, everything, context, w_qkv, w_other)
    w_mine = lax.all_to_all(w_wide, RING, 0, 0, tiled=True)
    pieces = [made[0]]
    for i in range(1, 8):
        step, side = i // 2, i % 2
        perm = [
            (s * 2 + c, (s + step) % 4 * 2 + (c + side) % 2) for s in range(4) for c in range(2)
        ]
        pieces.append(lax.ppermute(made[i], ("section", "core"), perm))
    starts = jnp.arange(8, dtype=jnp.int32)
    starts = (core + starts) % 2 * 4 + (section - starts // 2) % 4
    attn = attend(pieces, starts, seen, bounds)
    attn, w_mine = lax.optimization_barrier((attn, w_mine))
    w_theirs = lax.ppermute(w_mine, "core", SWAP)
    attn = lax.all_to_all(attn.reshape(16, rows, inner), SEQ, 0, 0, tiled=True)
    attn, stored_attn = lax.optimization_barrier((attn, stored_attn))
    stored = lax.all_to_all(stored_attn.reshape(8, 2 * rows, inner), RING, 0, 0, tiled=True)
    attn = attn.reshape(8, 2, rows, inner)
    mine = lax.dynamic_index_in_dim(attn, core, 1, keepdims=False)
    theirs = lax.dynamic_index_in_dim(attn, 1 - core, 1, keepdims=False)
    branch = jnp.einsum(
        "hri,hic->rc", mine, w_mine, preferred_element_type=jnp.float32
    ) + jnp.einsum("hri,hic->rc", theirs, w_theirs, preferred_element_type=jnp.float32)
    held = pending[0].astype(jnp.float32) + with_context * context[0][None, :]
    source = jnp.where(is_generator, latent[0].astype(jnp.float32), held)
    block_out = (source + branch).astype(jnp.bfloat16)[None, None]
    return (block_out,) + gradients(own_weight, branch, stored)


def gradients(own_weight, branch, stored):
    rows, width = branch.shape
    sections = lax.axis_size("section")
    section, core = lax.axis_index("section"), lax.axis_index("core")
    part = width // sections
    terms = (own_weight * branch).astype(jnp.bfloat16)
    total = None
    for step in (2, 1, 3, 0):
        column = (section + step) % sections * part
        term = lax.dynamic_slice_in_dim(terms, column, part, 1)
        if step:
            term = lax.ppermute(term, "section", moved("section", sections, step))
        total = term.astype(jnp.float32) + (0.0 if total is None else total)
    grad_bf = total.astype(jnp.bfloat16)
    other = lax.ppermute(grad_bf, "core", SWAP)
    both = jnp.where(core == 0, jnp.stack([grad_bf, other]), jnp.stack([other, grad_bf]))
    both = both.reshape(2 * rows, part)
    inner = stored.shape[2]
    product = jnp.einsum("hri,rc->hic", stored, both, preferred_element_type=jnp.float32)
    product = product.astype(jnp.bfloat16).reshape(16, inner // 2, part)
    product = lax.all_to_all(product, RING + ("dp",), 0, 0, tiled=True)
    summed = jnp.sum(product.astype(jnp.float32), axis=0).astype(jnp.bfloat16)
    summed = jnp.broadcast_to(summed[None], (8,) + summed.shape)
    summed = lax.all_to_all(summed, ("section", "dp"), 0, 0, tiled=True)
    grad_out = summed.reshape(4, 2, inner // 2, part).transpose(1, 2, 0, 3)
    grad_out = grad_out.reshape(inner, width).astype(jnp.float32)
    groups, starts = [grad_bf], [section * part]
    for step in (2, 1, 3):
        groups.append(lax.ppermute(grad_bf, "section", moved("section", sections, step)))
        starts.append((section - step) % sections * part)
    gradient = place_all(
        jnp.stack([jnp.stack([jnp.zeros_like(s), s]) for s in starts]), groups, (rows, width)
    )
    return (gradient[None], grad_out)


def solution(mesh):
    fine = Mesh(mesh.devices.reshape(4, 4, 2, 2, 2), ("section", "x", "zhi", "core", "dp"))
    placed = (
        P(),
        P(None, "dp", None),
        P("dp", SEQ, None),
        P("dp", SEQ, None),
        P("dp", None),
        P(None, None, SEQ),
        P(None, SEQ, None),
        P("dp", None, SEQ),
    )
    return jax.shard_map(
        per_device,
        mesh=fine,
        in_specs=placed,
        out_specs=(P("section", "dp", SEQ, None), P("dp", SEQ, None), P(SEQ, None)),
        check_vma=False,
    )
```

time: 327 us -> 250 us (0.76)
  waiting for transfers between devices: 143 us -> 77.5 us
  starting transfers between devices: 17 us -> 61.7 us
  blocking collectives: 63.7 us -> 22.4 us
  matrix products: 23.6 us -> 10.8 us
  between operations: 18 us -> 6.49 us
  Pallas kernels: 34.6 us -> 44.3 us
  local copies, waits for them, and re-layouts: 8.81 us -> 15.7 us
  other arithmetic: 14.8 us -> 8.92 us
    all_gather x2 -> x0, waiting for transfers between devices: 131 us -> none  [the longest x1 95.7 us: per_device(): lax.all_gather(normed, SEQ, axis=0, tiled=True)]
    ppermute x1 -> x25, waiting for transfers between devices: 1.49 us -> 63.8 us  [the longest x7 22.8 us: per_device(): pieces.append(lax.ppermute(made[i], ('section', 'core'), perm))]
    all_gather x2 -> x0, blocking collectives: 44.8 us -> none  [the longest x1 29.3 us: gradients(): lax.all_gather(total, ('section', 'dp'), axis=1, tiled=True)]
    ppermute x1 -> x25, starting transfers between devices: 0.08 us -> 35.4 us  [the longest x7 8.32 us: per_device(): pieces.append(lax.ppermute(made[i], ('section', 'core'), perm))]
    pallas_call x0 -> x2, Pallas kernels: none -> 19.1 us  [the longest x1 16.4 us: project(): pl.pallas_call(project_kernel, out_shape=[jax.ShapeDtypeStruct((many, col...]
    dot_general x2, matrix products: 21.6 us -> 8.74 us  [the longest x1 4.93 us: per_device(): jnp.einsum('hri,hic->rc', mine, w_mine, preferred_element_type=jnp.float32)]
    all_to_all x3 -> x4, starting transfers between devices: 16.8 us -> 26.3 us  [the longest x1 8.68 us: per_device(): w_mine = lax.all_to_all(w_wide, RING, 0, 0, tiled=True)]
    pallas_call x1, Pallas kernels: 34.6 us -> 25.2 us  [attend(): pl.pallas_call(attention_kernel, out_shape=jax.ShapeDtypeStruct((length,...]
  transfers between devices with their start and end apart: 6 -> 29, of which waited for: 5 -> 18; matrix products, arithmetic and copies ran while one was open for 8% -> 6% of each run, Pallas kernels for 11% -> 18%
where the time goes in v2:
time: 250 us; the launch traced here: 248 us
  waiting for transfers between devices  77.5 us (31%)
  starting transfers between devices  61.7 us (25%)
  Pallas kernels  44.3 us (18%)
  blocking collectives  22.4 us (9%)
  local copies, waits for them, and re-layouts  15.7 us (6%)
  matrix products  10.8 us (4%)
  other arithmetic  8.92 us (4%)
  between operations  6.49 us (3%)
    pallas_call x1, Pallas kernels, attend(): pl.pallas_call(attention_kernel, out_shape=jax.ShapeDtypeStruct((length,...  25.2 us
    ppermute x7, waiting for transfers between devices, per_device(): pieces.append(lax.ppermute(made[i], ('section', 'core'), perm))  22.8 us
    all_to_all x1, blocking collectives, gradients(): product = lax.all_to_all(product, RING + ('dp',), 0, 0, tiled=True)  22.4 us
    pallas_call x1, Pallas kernels, project(): pl.pallas_call(project_kernel, out_shape=[jax.ShapeDtypeStruct((many, col...  16.4 us
    ppermute x2, waiting for transfers between devices, per_device(): left = lax.ppermute(ours, 'x', moved('x', 4, 1))  14.9 us
    ppermute x3, waiting for transfers between devices, gradients(): lax.ppermute(grad_bf, 'section', moved('section', sections, step))  12 us
    all_to_all x1, starting transfers between devices, per_device(): w_mine = lax.all_to_all(w_wide, RING, 0, 0, tiled=True)  8.68 us
    all_to_all x1, waiting for transfers between devices, per_device(): attn = lax.all_to_all(attn.reshape(16, rows, inner), SEQ, 0, 0, tiled=True)  8.56 us
  transfers between devices with their start and end apart: 29, of which 18 were waited for; matrix products, arithmetic and copies ran while one was open for 6% of the time, Pallas kernels for 18%

profile of v2, /device:TPU:2, one launch (start us, length us, event | category | flops | bytes accessed | tf_op | source)
XLA Modules:
  0.0 247.8 jit_solution(13220267833909484842)
XLA Ops:
  3.5 3.9 %collective-permute-start.4 = (bf16[2,48,2560]{2,1,0:T(8,128)(2,1)S(1)}, bf16[2,48,2560]{2,1,0:T(8,128)(2,1)}, u32[]{:S(2)}, u32[]{:S(2)}) collective-permute-start(bf16[2,48,2560]{2,1,0:T(8,128)(2,1)S(1)} %pad_maximum_fusion.refs_0_), channel_id=1, source_target_pairs={{0,4},{4,0},{1,5},{5,1},{2,6},{6,2},{3,7},{7,3},{8,12},{12,8},{9,1... | collective-permute-start | bytes 1474568 | tf_op jit(solution)/shard_map/ppermute | solution.py:257
  9.3 5.7 %collective-permute-done.1.refs_4_ = bf16[2,48,2560]{2,1,0:T(8,128)(2,1)S(1)} collective-permute-done((bf16[2,48,2560]{2,1,0:T(8,128)(2,1)S(1)}, bf16[2,48,2560]{2,1,0:T(8,128)(2,1)S(1)}, u32[]{:S(2)}, u32[]{:S(2)}) %collective-permute-start.1) | collective-permute-done | bytes 491552 | tf_op jit(solution)/shard_map/ppermute | solution.py:260
  20.6 2.8 %collective-permute-start.5 = (bf16[2,48,2560]{2,1,0:T(8,128)(2,1)}, bf16[2,48,2560]{2,1,0:T(8,128)(2,1)S(1)}, u32[]{:S(2)}, u32[]{:S(2)}) collective-permute-start(bf16[2,48,2560]{2,1,0:T(8,128)(2,1)} %collective-permute-done.4.refs_5_), channel_id=1, source_target_pairs={{0,24},{8,0},{16,8},{24,16},{1,25},{9,1},{17,9},{25,17},{2,26},{10... | collective-permute-start | bytes 1474568 | tf_op jit(solution)/shard_map/ppermute | solution.py:261
  23.4 9.2 %collective-permute-done.6.refs_9_ = bf16[2,48,2560]{2,1,0:T(8,128)(2,1)S(1)} collective-permute-done((bf16[2,48,2560]{2,1,0:T(8,128)(2,1)}, bf16[2,48,2560]{2,1,0:T(8,128)(2,1)S(1)}, u32[]{:S(2)}, u32[]{:S(2)}) %collective-permute-start.6) | collective-permute-done | bytes 491552 | tf_op jit(solution)/shard_map/ppermute | solution.py:260
  39.7 4.2 %collective-permute-done.8.refs_8_ = bf16[48,2560]{1,0:T(8,128)(2,1)} collective-permute-done((bf16[48,2560]{1,0:T(8,128)(2,1)S(1)}, bf16[48,2560]{1,0:T(8,128)(2,1)}, u32[]{:S(2)}, u32[]{:S(2)}) %collective-permute-start.8) | collective-permute-done | bytes 245792 | tf_op jit(solution)/shard_map/ppermute | solution.py:263
  46.7 8.7 %all-to-all-start = ((bf16[8,128,2560]{2,1,0:T(8,128)(2,1)}), bf16[8,128,2560]{2,1,0:T(8,128)(2,1)}, u32[]{:S(2)}, u32[]{:S(2)}) async-start(bf16[8,128,2560]{2,1,0:T(8,128)(2,1)} %broadcast_in_dim.26), calls=%async_computation | async-start | bytes 10485760 | tf_op jit(solution)/shard_map/all_to_all | solution.py:274
  56.8 16.4 %project.1 = (bf16[384,384]{1,0:T(8,128)(2,1)}, bf16[384,384]{1,0:T(8,128)(2,1)}, bf16[384,384]{1,0:T(8,128)(2,1)}, bf16[384,384]{1,0:T(8,128)(2,1)}, bf16[384,3...) custom-call(s32[12]{0:T(128)} %pad_add_fusion.7.place, ...), custom_call_target="tpu_custom_call" | custom-call | tf_op jit(solution)/shard_map/project/pallas_call | solution.py:187
  75.1 3.8 %convert_reduce_fusion = s32[3072]{0:T(1024)S(1)} fusion(s32[3072]{0:T(1024)S(1)} %bitcast.87), kind=kLoop, calls=%fused_computation | loop fusion | flops 28308480 | bytes 24576 | tf_op jit(solution)/shard_map/reduce_sum | solution.py:104
  88.3 3.7 %collective-permute-done.12.refs_3_ = bf16[384,384]{1,0:T(8,128)(2,1)S(1)} collective-permute-done((bf16[384,384]{1,0:T(8,128)(2,1)}, bf16[384,384]{1,0:T(8,128)(2,1)S(1)}, u32[]{:S(2)}, u32[]{:S(2)}) %collective-permute-start.12) | collective-permute-done | bytes 294944 | tf_op jit(solution)/shard_map/ppermute | solution.py:281
  92.0 6.5 %collective-permute-done.13.refs_4_ = bf16[384,384]{1,0:T(8,128)(2,1)S(1)} collective-permute-done((bf16[384,384]{1,0:T(8,128)(2,1)}, bf16[384,384]{1,0:T(8,128)(2,1)S(1)}, u32[]{:S(2)}, u32[]{:S(2)}) %collective-permute-start.13) | collective-permute-done | bytes 294944 | tf_op jit(solution)/shard_map/ppermute | solution.py:281
  98.5 5.6 %collective-permute-done.14.refs_5_ = bf16[384,384]{1,0:T(8,128)(2,1)S(1)} collective-permute-done((bf16[384,384]{1,0:T(8,128)(2,1)}, bf16[384,384]{1,0:T(8,128)(2,1)S(1)}, u32[]{:S(2)}, u32[]{:S(2)}) %collective-permute-start.14) | collective-permute-done | bytes 294944 | tf_op jit(solution)/shard_map/ppermute | solution.py:281
  105.6 5.5 %collective-permute-done.16.refs_7_ = bf16[384,384]{1,0:T(8,128)(2,1)} collective-permute-done((bf16[384,384]{1,0:T(8,128)(2,1)}, bf16[384,384]{1,0:T(8,128)(2,1)}, u32[]{:S(2)}, u32[]{:S(2)}) %collective-permute-start.16) | collective-permute-done | bytes 294944 | tf_op jit(solution)/shard_map/ppermute | solution.py:281
  111.2 25.2 %attend.1 = bf16[3072,128]{1,0:T(8,128)(2,1)} custom-call(s32[6,2]{1,0:T(8,128)} %pad_add_fusion.bounds, s32[8]{0:T(128)} %fusion.15.starts, bf16[384,384]{1,0:T(8,128)(2,1)} %get-tuple-element.36.refs_0_, bf16[384,384]{1,0:T(8,128)(2,1)} %copy-done.10, bf16[384,384]{1,0:T(8,128)(2,1)} %copy-done.11, bf16[384,384]{1,0:T(8,128)(2,1)} %copy-done.12, ...), custom_call_target="tpu_custom_call" | custom-call | tf_op jit(solution)/shard_map/attend/pallas_call | solution.py:116
  137.0 7.2 %all-to-all-start.1 = ((bf16[16,192,128]{2,1,0:T(8,128)(2,1)}), bf16[16,192,128]{2,1,0:T(8,128)(2,1)S(1)}, u32[]{:S(2)}, u32[]{:S(2)}) async-start(bf16[16,192,128]{2,1,0:T(8,128)(2,1)} %bitcast.78), calls=%async_computation.1 | async-start | bytes 1572864 | tf_op jit(solution)/shard_map/all_to_all | solution.py:287
  148.4 8.6 %all-to-all-done.1 = bf16[16,192,128]{2,1,0:T(8,128)(2,1)S(1)} async-done(((bf16[16,192,128]{2,1,0:T(8,128)(2,1)}), bf16[16,192,128]{2,1,0:T(8,128)(2,1)S(1)}, u32[]{:S(2)}, u32[]{:S(2)}) %all-to-all-start.1) | async-done | bytes 786464 | tf_op jit(solution)/shard_map/all_to_all | solution.py:287
  157.9 3.8 %convolution_bitcast_fusion = f32[192,2560]{1,0:T(8,128)S(1)} fusion(bf16[8,128,2560]{2,1,0:T(8,128)(2,1)} %collective-permute-done.17, bf16[8,2,192,128]{3,2,1,0:T(8,128)(2,1)S(1)} %bitcast.76, s32[]{:T(128)S(6)} %select_n.182), kind=kOutput, calls=%fused_computation.1 | convolution fusion | flops 1006632960 | bytes 7602180 | tf_op jit(solution)/shard_map/hri,hic->rc/dot_general | solution.py:295
  161.7 4.9 %multiply_convert_fusion = (bf16[192,2560]{1,0:T(8,128)(2,1)S(1)}, bf16[1,1,192,2560]{3,2,1,0:T(8,128)(2,1)}) fusion(f32[]{:T(128)S(6)} %select_n.188, f32[2560]{0:T(1024)S(1)} %multiply_reduce_fusion, bf16[1,192,2560]{2,1,0:T(8,128)(2,1)S(1)} %copy-done.4, bf16[1,192,2560]{2,1,0:T(8,128)(2,1)S(1)} %copy-done.5, pred[]{:T(512)S(6)} %eq.32, ...), kind=kOutput, calls=%fused_computation.8 | convolution fusion | flops 1011056640 | bytes 11544585 | tf_op jit(solution)/shard_map/hri,hic->rc/dot_general | solution.py:293
  174.6 6.8 %all-to-all-start.2 = ((bf16[8,384,128]{1,2,0:T(8,128)(2,1)}), bf16[8,384,128]{1,2,0:T(8,128)(2,1)}, u32[]{:S(2)}, u32[]{:S(2)}) async-start(bf16[8,384,128]{1,2,0:T(8,128)(2,1)} %copy.39), calls=%async_computation.2 | async-start | bytes 1572864 | tf_op jit(solution)/shard_map/all_to_all | solution.py:289
  187.1 5.1 %all-to-all-done.2 = bf16[8,384,128]{1,2,0:T(8,128)(2,1)} async-done(((bf16[8,384,128]{1,2,0:T(8,128)(2,1)}), bf16[8,384,128]{1,2,0:T(8,128)(2,1)}, u32[]{:S(2)}, u32[]{:S(2)}) %all-to-all-start.2) | async-done | bytes 786464 | tf_op jit(solution)/shard_map/all_to_all | solution.py:289
  194.3 22.4 %all_to_all.25 = bf16[16,64,640]{2,1,0:T(8,128)(2,1)S(1)} all-to-all(bf16[16,64,640]{2,1,0:T(8,128)(2,1)S(1)} %bitcast.74), channel_id=1, replica_groups=mesh['section'=4,'x'=4,'zhi'=2,'core'=2,'dp'=2] {'x','zhi','dp'}, dimensions={0} | all-to-all | bytes 2621440 | tf_op jit(solution)/shard_map/all_to_all | solution.py:322
  219.3 3.5 %all-to-all-start.4 = ((bf16[8,64,640]{2,1,0:T(8,128)(2,1)}), bf16[8,64,640]{2,1,0:T(8,128)(2,1)S(1)}, u32[]{:S(2)}, u32[]{:S(2)}) async-start(bf16[8,64,640]{2,1,0:T(8,128)(2,1)} %broadcast_in_dim.30), calls=%async_computation.4 | async-start | bytes 1310720 | tf_op jit(solution)/shard_map/all_to_all | solution.py:325
  222.9 3.4 %collective-permute-start.21 = (bf16[192,640]{1,0:T(8,128)(2,1)S(1)}, bf16[192,640]{1,0:T(8,128)(2,1)S(1)}, u32[]{:S(2)}, u32[]{:S(2)}) collective-permute-start(bf16[192,640]{1,0:T(8,128)(2,1)S(1)} %add_convert_fusion.refs_0_), channel_id=1, source_target_pairs={{0,64},{32,96},{64,0},{96,32},{1,65},{33,97},{65,1},{97,33},{2,66}... | collective-permute-start | bytes 737288 | tf_op jit(solution)/shard_map/ppermute | solution.py:330
  230.3 9.4 %collective-permute-done.21.refs_1_ = bf16[192,640]{1,0:T(8,128)(2,1)S(1)} collective-permute-done((bf16[192,640]{1,0:T(8,128)(2,1)S(1)}, bf16[192,640]{1,0:T(8,128)(2,1)S(1)}, u32[]{:S(2)}, u32[]{:S(2)}) %collective-permute-start.21) | collective-permute-done | bytes 245792 | tf_op jit(solution)/shard_map/ppermute | solution.py:330
  243.0 2.7 %place_all.1 = f32[192,2560]{1,0:T(8,128)} custom-call(s32[4,2]{1,0:T(4,128)} %pad_add_fusion.1.starts, bf16[192,640]{1,0:T(8,128)(2,1)} %copy-done.2, bf16[192,640]{1,0:T(8,128)(2,1)} %copy-done.15, bf16[192,640]{1,0:T(8,128)(2,1)} %copy-done.16, bf16[192,640]{1,0:T(8,128)(2,1)} %collective-permute-done.23.refs_3_), custom_call_target="tpu_custom_call" | custom-call | tf_op jit(solution)/shard_map/place_all/pallas_call | solution.py:215
  (114 shorter events, 62.3 us)
Async XLA Ops:
  2.0 13.0 %collective-permute-start.1 = (bf16[2,48,2560]{2,1,0:T(8,128)(2,1)S(1)}, bf16[2,48,2560]{2,1,0:T(8,128)(2,1)S(1)}, u32[]{:S(2)}, u32[]{:S(2)}) collective-permute-start(bf16[2,48,2560]{2,1,0:T(8,128)(2,1)S(1)} %pad_maximum_fusion.refs_0_), channel_id=1, source_target_pairs={{0,8},{8,16},{16,24},{24,0},{1,9},{9,17},{17,25},{25,1},{2,10},{10... | collective-permute-start | bytes 1474568 | tf_op jit(solution)/shard_map/ppermute | solution.py:260
  3.5 14.9 %collective-permute-start.4 = (bf16[2,48,2560]{2,1,0:T(8,128)(2,1)S(1)}, bf16[2,48,2560]{2,1,0:T(8,128)(2,1)}, u32[]{:S(2)}, u32[]{:S(2)}) collective-permute-start(bf16[2,48,2560]{2,1,0:T(8,128)(2,1)S(1)} %pad_maximum_fusion.refs_0_), channel_id=1, source_target_pairs={{0,4},{4,0},{1,5},{5,1},{2,6},{6,2},{3,7},{7,3},{8,12},{12,8},{9,1... | collective-permute-start | bytes 1474568 | tf_op jit(solution)/shard_map/ppermute | solution.py:257
  7.9 48.9 %collective-permute-start.9 = (bf16[3,2560,384]{2,1,0:T(8,128)(2,1)}, bf16[3,2560,384]{2,1,0:T(8,128)(2,1)}, u32[]{:S(2)}, u32[]{:S(2)}) collective-permute-start(bf16[3,2560,384]{2,1,0:T(8,128)(2,1)} %refs_11_.1), channel_id=1, source_target_pairs={{0,2},{2,0},{1,3},{3,1},{4,6},{6,4},{5,7},{7,5},{8,10},{10,8},{9,1... | collective-permute-start | bytes 17694728 | tf_op jit(solution)/shard_map/ppermute | solution.py:266
  15.0 23.7 %collective-permute-start.2 = (bf16[48,2560]{1,0:T(8,128)(2,1)S(1)}, bf16[48,2560]{1,0:T(8,128)(2,1)}, u32[]{:S(2)}, u32[]{:S(2)}) collective-permute-start(bf16[48,2560]{1,0:T(8,128)(2,1)S(1)} %slice_bitcast_fusion.3), channel_id=1, source_target_pairs={{0,8},{8,16},{16,24},{24,0},{1,9},{9,17},{17,25},{25,1},{2,10},{10... | collective-permute-start | bytes 737288 | tf_op jit(solution)/shard_map/ppermute | solution.py:262
  18.5 14.1 %collective-permute-start.6 = (bf16[2,48,2560]{2,1,0:T(8,128)(2,1)}, bf16[2,48,2560]{2,1,0:T(8,128)(2,1)S(1)}, u32[]{:S(2)}, u32[]{:S(2)}) collective-permute-start(bf16[2,48,2560]{2,1,0:T(8,128)(2,1)} %collective-permute-done.4.refs_5_), channel_id=1, source_target_pairs={{0,8},{8,16},{16,24},{24,0},{1,9},{9,17},{17,25},{25,1},{2,10},{10... | collective-permute-start | bytes 1474568 | tf_op jit(solution)/shard_map/ppermute | solution.py:260
  19.8 18.9 %collective-permute-start.3 = (bf16[48,2560]{1,0:T(8,128)(2,1)S(1)}, bf16[48,2560]{1,0:T(8,128)(2,1)}, u32[]{:S(2)}, u32[]{:S(2)}) collective-permute-start(bf16[48,2560]{1,0:T(8,128)(2,1)S(1)} %slice_bitcast_fusion.2), channel_id=1, source_target_pairs={{0,24},{8,0},{16,8},{24,16},{1,25},{9,1},{17,9},{25,17},{2,26},{10... | collective-permute-start | bytes 737288 | tf_op jit(solution)/shard_map/ppermute | solution.py:263
  20.6 16.3 %collective-permute-start.5 = (bf16[2,48,2560]{2,1,0:T(8,128)(2,1)}, bf16[2,48,2560]{2,1,0:T(8,128)(2,1)S(1)}, u32[]{:S(2)}, u32[]{:S(2)}) collective-permute-start(bf16[2,48,2560]{2,1,0:T(8,128)(2,1)} %collective-permute-done.4.refs_5_), channel_id=1, source_target_pairs={{0,24},{8,0},{16,8},{24,16},{1,25},{9,1},{17,9},{25,17},{2,26},{10... | collective-permute-start | bytes 1474568 | tf_op jit(solution)/shard_map/ppermute | solution.py:261
  46.7 89.7 %all-to-all-start = ((bf16[8,128,2560]{2,1,0:T(8,128)(2,1)}), bf16[8,128,2560]{2,1,0:T(8,128)(2,1)}, u32[]{:S(2)}, u32[]{:S(2)}) async-start(bf16[8,128,2560]{2,1,0:T(8,128)(2,1)} %broadcast_in_dim.26), calls=%async_computation | async-start | bytes 10485760 | tf_op jit(solution)/shard_map/all_to_all | solution.py:274
  73.2 12.5 %collective-permute-start.10 = (bf16[384,384]{1,0:T(8,128)(2,1)}, bf16[384,384]{1,0:T(8,128)(2,1)S(1)}, u32[]{:S(2)}, u32[]{:S(2)}) collective-permute-start(bf16[384,384]{1,0:T(8,128)(2,1)} %get-tuple-element.37), channel_id=1, source_target_pairs={{0,2},{2,0},{32,34},{34,32},{64,66},{66,64},{96,98},{98,96},{1,3},... | collective-permute-start | bytes 884744 | tf_op jit(solution)/shard_map/ppermute | solution.py:281
  73.3 14.1 %collective-permute-start.11 = (bf16[384,384]{1,0:T(8,128)(2,1)}, bf16[384,384]{1,0:T(8,128)(2,1)S(1)}, u32[]{:S(2)}, u32[]{:S(2)}) collective-permute-start(bf16[384,384]{1,0:T(8,128)(2,1)} %get-tuple-element.38), channel_id=1, source_target_pairs={{0,32},{2,34},{32,64},{34,66},{64,96},{66,98},{96,0},{98,2},{1,33}... | collective-permute-start | bytes 884744 | tf_op jit(solution)/shard_map/ppermute | solution.py:281
  82.3 16.2 %collective-permute-start.13 = (bf16[384,384]{1,0:T(8,128)(2,1)}, bf16[384,384]{1,0:T(8,128)(2,1)S(1)}, u32[]{:S(2)}, u32[]{:S(2)}) collective-permute-start(bf16[384,384]{1,0:T(8,128)(2,1)} %get-tuple-element.40), channel_id=1, source_target_pairs={{0,64},{2,66},{32,96},{34,98},{64,0},{66,2},{96,32},{98,34},{1,65}... | collective-permute-start | bytes 884744 | tf_op jit(solution)/shard_map/ppermute | solution.py:281
  84.0 20.1 %collective-permute-start.14 = (bf16[384,384]{1,0:T(8,128)(2,1)}, bf16[384,384]{1,0:T(8,128)(2,1)S(1)}, u32[]{:S(2)}, u32[]{:S(2)}) collective-permute-start(bf16[384,384]{1,0:T(8,128)(2,1)} %get-tuple-element.41), channel_id=1, source_target_pairs={{0,66},{2,64},{32,98},{34,96},{64,2},{66,0},{96,34},{98,32},{1,67}... | collective-permute-start | bytes 884744 | tf_op jit(solution)/shard_map/ppermute | solution.py:281
  85.7 20.0 %collective-permute-start.15 = (bf16[384,384]{1,0:T(8,128)(2,1)}, bf16[384,384]{1,0:T(8,128)(2,1)}, u32[]{:S(2)}, u32[]{:S(2)}) collective-permute-start(bf16[384,384]{1,0:T(8,128)(2,1)} %get-tuple-element.42), channel_id=1, source_target_pairs={{0,96},{2,98},{32,0},{34,2},{64,32},{66,34},{96,64},{98,66},{1,97}... | collective-permute-start | bytes 884744 | tf_op jit(solution)/shard_map/ppermute | solution.py:281
  87.3 23.8 %collective-permute-start.16 = (bf16[384,384]{1,0:T(8,128)(2,1)}, bf16[384,384]{1,0:T(8,128)(2,1)}, u32[]{:S(2)}, u32[]{:S(2)}) collective-permute-start(bf16[384,384]{1,0:T(8,128)(2,1)} %get-tuple-element.43), channel_id=1, source_target_pairs={{0,98},{2,96},{32,2},{34,0},{64,34},{66,32},{96,66},{98,64},{1,99}... | collective-permute-start | bytes 884744 | tf_op jit(solution)/shard_map/ppermute | solution.py:281
  136.4 20.6 %collective-permute-start.17 = (bf16[8,128,2560]{2,1,0:T(8,128)(2,1)}, bf16[8,128,2560]{2,1,0:T(8,128)(2,1)}, u32[]{:S(2)}, u32[]{:S(2)}) collective-permute-start(bf16[8,128,2560]{2,1,0:T(8,128)(2,1)} %all-to-all-done), channel_id=1, source_target_pairs={{0,2},{2,0},{1,3},{3,1},{4,6},{6,4},{5,7},{7,5},{8,10},{10,8},{9,1... | collective-permute-start | bytes 15728648 | tf_op jit(solution)/shard_map/ppermute | solution.py:286
  137.0 20.0 %all-to-all-start.1 = ((bf16[16,192,128]{2,1,0:T(8,128)(2,1)}), bf16[16,192,128]{2,1,0:T(8,128)(2,1)S(1)}, u32[]{:S(2)}, u32[]{:S(2)}) async-start(bf16[16,192,128]{2,1,0:T(8,128)(2,1)} %bitcast.78), calls=%async_computation.1 | async-start | bytes 1572864 | tf_op jit(solution)/shard_map/all_to_all | solution.py:287
  167.4 14.0 %collective-permute-start.18 = (bf16[192,640]{1,0:T(8,128)(2,1)}, bf16[192,640]{1,0:T(8,128)(2,1)}, u32[]{:S(2)}, u32[]{:S(2)}) collective-permute-start(bf16[192,640]{1,0:T(8,128)(2,1)} %get-tuple-element.51), channel_id=1, source_target_pairs={{0,96},{32,0},{64,32},{96,64},{1,97},{33,1},{65,33},{97,65},{2,98}... | collective-permute-start | bytes 737288 | tf_op jit(solution)/shard_map/ppermute | solution.py:313
  169.9 14.2 %collective-permute-start.19 = (bf16[192,640]{1,0:T(8,128)(2,1)S(1)}, bf16[192,640]{1,0:T(8,128)(2,1)}, u32[]{:S(2)}, u32[]{:S(2)}) collective-permute-start(bf16[192,640]{1,0:T(8,128)(2,1)S(1)} %get-tuple-element.53), channel_id=1, source_target_pairs={{0,32},{32,64},{64,96},{96,0},{1,33},{33,65},{65,97},{97,1},{2,34}... | collective-permute-start | bytes 737288 | tf_op jit(solution)/shard_map/ppermute | solution.py:313
  169.9 14.2 %collective-permute-start.20 = (bf16[192,640]{1,0:T(8,128)(2,1)S(1)}, bf16[192,640]{1,0:T(8,128)(2,1)}, u32[]{:S(2)}, u32[]{:S(2)}) collective-permute-start(bf16[192,640]{1,0:T(8,128)(2,1)S(1)} %get-tuple-element.52), channel_id=1, source_target_pairs={{0,64},{32,96},{64,0},{96,32},{1,65},{33,97},{65,1},{97,33},{2,66}... | collective-permute-start | bytes 737288 | tf_op jit(solution)/shard_map/ppermute | solution.py:313
  174.6 17.7 %all-to-all-start.2 = ((bf16[8,384,128]{1,2,0:T(8,128)(2,1)}), bf16[8,384,128]{1,2,0:T(8,128)(2,1)}, u32[]{:S(2)}, u32[]{:S(2)}) async-start(bf16[8,384,128]{1,2,0:T(8,128)(2,1)} %copy.39), calls=%async_computation.2 | async-start | bytes 1572864 | tf_op jit(solution)/shard_map/all_to_all | solution.py:289
  219.3 26.4 %all-to-all-start.4 = ((bf16[8,64,640]{2,1,0:T(8,128)(2,1)}), bf16[8,64,640]{2,1,0:T(8,128)(2,1)S(1)}, u32[]{:S(2)}, u32[]{:S(2)}) async-start(bf16[8,64,640]{2,1,0:T(8,128)(2,1)} %broadcast_in_dim.30), calls=%async_computation.4 | async-start | bytes 1310720 | tf_op jit(solution)/shard_map/all_to_all | solution.py:325
  222.9 16.7 %collective-permute-start.21 = (bf16[192,640]{1,0:T(8,128)(2,1)S(1)}, bf16[192,640]{1,0:T(8,128)(2,1)S(1)}, u32[]{:S(2)}, u32[]{:S(2)}) collective-permute-start(bf16[192,640]{1,0:T(8,128)(2,1)S(1)} %add_convert_fusion.refs_0_), channel_id=1, source_target_pairs={{0,64},{32,96},{64,0},{96,32},{1,65},{33,97},{65,1},{97,33},{2,66}... | collective-permute-start | bytes 737288 | tf_op jit(solution)/shard_map/ppermute | solution.py:330
  226.3 16.0 %collective-permute-start.22 = (bf16[192,640]{1,0:T(8,128)(2,1)S(1)}, bf16[192,640]{1,0:T(8,128)(2,1)S(1)}, u32[]{:S(2)}, u32[]{:S(2)}) collective-permute-start(bf16[192,640]{1,0:T(8,128)(2,1)S(1)} %add_convert_fusion.refs_0_), channel_id=1, source_target_pairs={{0,32},{32,64},{64,96},{96,0},{1,33},{33,65},{65,97},{97,1},{2,34}... | collective-permute-start | bytes 737288 | tf_op jit(solution)/shard_map/ppermute | solution.py:330
  226.9 15.4 %collective-permute-start.23 = (bf16[192,640]{1,0:T(8,128)(2,1)S(1)}, bf16[192,640]{1,0:T(8,128)(2,1)}, u32[]{:S(2)}, u32[]{:S(2)}) collective-permute-start(bf16[192,640]{1,0:T(8,128)(2,1)S(1)} %add_convert_fusion.refs_0_), channel_id=1, source_target_pairs={{0,96},{32,0},{64,32},{96,64},{1,97},{33,1},{65,33},{97,65},{2,98}... | collective-permute-start | bytes 737288 | tf_op jit(solution)/shard_map/ppermute | solution.py:330
  (25 other events, 380.6 us)

commit v3 on v2

--- a/solution.py
+++ b/solution.py
@@ -21,19 +21,19 @@
 
 
 def attention_kernel(bounds, starts, *refs):
-    pieces = refs[:8]
-    seen, out, qkv, values, top, acc, sems = refs[8:]
+    pieces = refs[:16]
+    seen, out, qkv, values, top, acc, sems = refs[16:]
     tile = pl.program_id(0)
     length = qkv.shape[0]
-    chips = 8
-    chunk = pieces[0].shape[0] // chips
+    ring = 4
+    chunk = pieces[0].shape[0] // ring
 
     @pl.when(tile == 0)
     def _():
         copies = []
         for i, piece in enumerate(pieces):
-            for b in range(chips):
-                place = pl.multiple_of(starts[i] * chunk + b * (length // chips), chunk)
+            for b in range(ring):
+                place = pl.multiple_of(starts[i] * chunk + b * (length // ring), chunk)
                 copies.append(
                     pltpu.make_async_copy(
                         piece.at[pl.ds(b * chunk, chunk)],
@@ -119,7 +119,7 @@
         grid_spec=pltpu.PrefetchScalarGridSpec(
             num_scalar_prefetch=2,
             grid=(length // QUERY_TILE,),
-            in_specs=[pl.BlockSpec(memory_space=pl.ANY)] * 8
+            in_specs=[pl.BlockSpec(memory_space=pl.ANY)] * 16
             + [pl.BlockSpec((QUERY_TILE, 1), lambda i, b, s: (i, 0))],
             out_specs=pl.BlockSpec((QUERY_TILE, HEAD_DIM), lambda i, b, s: (i, 0)),
             scratch_shapes=[
@@ -127,7 +127,7 @@
                 pltpu.VMEM((length, 2 * HEAD_DIM), jnp.bfloat16),
                 pltpu.VMEM((parts, QUERY_PART, 1), jnp.float32),
                 pltpu.VMEM((parts, QUERY_PART, 2 * HEAD_DIM), jnp.float32),
-                pltpu.SemaphoreType.DMA((8, 8)),
+                pltpu.SemaphoreType.DMA((16, 4)),
             ],
         ),
         name="attend",
@@ -135,52 +135,51 @@
 
 
 def project_kernel(place, *refs):
-    rows = refs[:10]
-    context, w_mine, w_other = refs[10:13]
-    outs, (sources, scales) = refs[13:21], refs[21:]
+    own, right, far_scored, far_latent, left, context, w_mine, w_other = refs[:8]
+    outs, rows = refs[8:16], refs[16]
     step = pl.program_id(0)
-    chunk = rows[0].shape[1]
+    chunk = own.shape[1]
 
     @pl.when(step == 0)
     def _():
-        added = context[...]
-        for side in range(2):
-            own, right, far_scored, far_latent, left = rows[side * 5 : side * 5 + 5]
-            found = [(own[0], own[1]), (right[0], right[1])]
-            found += [(far_scored[...], far_latent[...]), (left[0], left[1])]
-            for i, (scored, latent) in enumerate(found):
-                at = pl.ds(pl.multiple_of(place[4 + side * 4 + i] * chunk, chunk), chunk)
-                wide = scored.astype(jnp.float32)
-                shifted = wide + added
-                sources[0, at, :] = scored
-                sources[1, at, :] = shifted.astype(jnp.bfloat16)
-                sources[2, at, :] = latent
-                for j, v in enumerate((wide, shifted, latent.astype(jnp.float32))):
-                    scales[j, at, :] = lax.rsqrt(
-                        jnp.mean(v * v, axis=1, keepdims=True) + EPSILON
-                    )
+        found = [(own[0], own[1]), (right[0], right[1])]
+        found += [(far_scored[...], far_latent[...]), (left[0], left[1])]
+        for i, pair in enumerate(found):
+            at = pl.ds(pl.multiple_of(place[4 + i] * chunk, chunk), chunk)
+            for j in range(2):
+                rows[j, at, :] = pair[j]
 
     role = place[step]
-    kind = jnp.where(role == 0, 2, role % 2)
-    left = sources[kind]
-    scale = scales[kind]
+    source = rows[(role == 0).astype(jnp.int32)].astype(jnp.float32)
+    source = source + context[...] * (role % 2).astype(jnp.float32)
+    scale = lax.rsqrt(jnp.mean(source * source, axis=1, keepdims=True) + EPSILON)
+    source = source.astype(jnp.bfloat16)
+    columns = [
+        w_mine[0, :, : 2 * HEAD_DIM],
+        jnp.concatenate([w_mine[0, :, 2 * HEAD_DIM :], w_other[0, :, :HEAD_DIM]], axis=1),
+        w_other[0, :, HEAD_DIM:],
+    ]
     made = [
-        jnp.dot(left, weights[0], preferred_element_type=jnp.float32) * scale
-        for weights in (w_mine, w_other)
+        jnp.dot(source, weights, preferred_element_type=jnp.float32) * scale for weights in columns
     ]
+    queries = [made[0][:, :HEAD_DIM], made[1][:, HEAD_DIM:]]
+    others = [[made[0][:, HEAD_DIM:], made[1][:, :HEAD_DIM]], [made[2]]]
     for i in range(4):
 
         @pl.when(step == i)
         def _():
             for side in range(2):
                 out = outs[2 * i + side]
-                out[:, :HEAD_DIM] = (made[side][:, :HEAD_DIM] * SCORE_SCALE).astype(jnp.bfloat16)
-                out[:, HEAD_DIM:] = made[side][:, HEAD_DIM:].astype(jnp.bfloat16)
+                out[:, :HEAD_DIM] = (queries[side] * SCORE_SCALE).astype(jnp.bfloat16)
+                at = HEAD_DIM
+                for part in others[side]:
+                    out[:, at : at + part.shape[1]] = part.astype(jnp.bfloat16)
+                    at += part.shape[1]
 
 
 def project(place, rows, context, w_mine, w_other):
     chunk, width = rows[0].shape[1:]
-    many = 8 * chunk
+    many = 4 * chunk
     columns = w_mine.shape[2]
     picked = pl.BlockSpec((1, width, columns), lambda t, r: ((r[t] + 1) // 2, 0, 0))
     whole = pl.BlockSpec(memory_space=pltpu.VMEM)
@@ -190,15 +189,60 @@
         grid_spec=pltpu.PrefetchScalarGridSpec(
             num_scalar_prefetch=1,
             grid=(4,),
-            in_specs=[whole] * 11 + [picked, picked],
+            in_specs=[whole] * 6 + [picked, picked],
             out_specs=[pl.BlockSpec((many, columns), lambda t, r: (0, 0))] * 8,
-            scratch_shapes=[
-                pltpu.VMEM((3, many, width), jnp.bfloat16),
-                pltpu.VMEM((3, many, 1), jnp.float32),
-            ],
+            scratch_shapes=[pltpu.VMEM((2, many, width), jnp.bfloat16)],
         ),
         name="project",
     )(place, *rows, context, w_mine, w_other)
+
+
+def finish_kernel(place, *refs):
+    attn, pending, latent, context = refs[:4]
+    weights, block, terms = refs[4:20], refs[20], refs[21:]
+    step = pl.program_id(0)
+    branch = None
+    for i in range(0, 16, 2):
+        left = jnp.concatenate([attn[place[i]], attn[place[i + 1]]], axis=1)
+        right = jnp.concatenate([weights[i][...], weights[i + 1][...]], axis=0)
+        part = jnp.dot(left, right, preferred_element_type=jnp.float32)
+        branch = part if branch is None else branch + part
+    role = place[20]
+    scored = pending[...].astype(jnp.float32) + context[...] * (role % 2).astype(jnp.float32)
+    source = jnp.where(role == 0, latent[...].astype(jnp.float32), scored)
+    block[...] = (source + branch).astype(jnp.bfloat16)
+    weight = jnp.where(role == 2, GUIDE - 1.0, jnp.where(role == 3, 1.0, 0.0))
+    weight = jnp.where(role == 1, -GUIDE, weight)
+    for i, term in enumerate(terms):
+
+        @pl.when(step == i)
+        def _():
+            term[...] = (weight * branch).astype(jnp.bfloat16)
+
+
+def finish(place, attn, pending, latent, context, weights):
+    rows, width = pending.shape
+    inner = weights[0].shape[0]
+    part = width // 4
+    columns = pl.BlockSpec((rows, part), lambda t, s: (0, s[16 + t]))
+    return pl.pallas_call(
+        finish_kernel,
+        out_shape=[jax.ShapeDtypeStruct((rows, width), jnp.bfloat16)]
+        + [jax.ShapeDtypeStruct((rows, part), jnp.bfloat16)] * 4,
+        grid_spec=pltpu.PrefetchScalarGridSpec(
+            num_scalar_prefetch=1,
+            grid=(4,),
+            in_specs=[
+                pl.BlockSpec(memory_space=pltpu.VMEM),
+                columns,
+                columns,
+                pl.BlockSpec((1, part), lambda t, s: (0, s[16 + t])),
+            ]
+            + [pl.BlockSpec((inner, part), lambda t, s: (0, s[16 + t]))] * 16,
+            out_specs=[columns] + [pl.BlockSpec((rows, part), lambda t, s: (0, 0))] * 4,
+        ),
+        name="finish",
+    )(place, attn, pending, latent, context, *weights)
 
 
 def place_kernel(starts, *refs):
@@ -232,13 +276,7 @@
 def per_device(roles, block_ids, latent, pending, context, w_qkv, w_out, stored_attn):
     section, core = lax.axis_index("section"), lax.axis_index("core")
     section_role = lax.dynamic_index_in_dim(roles, section, 0, keepdims=False)
-    own_weight = jnp.where(
-        section_role == 1,
-        -GUIDE,
-        jnp.where(section_role == 2, GUIDE - 1.0, jnp.where(section_role == 3, 1.0, 0.0)),
-    )
     is_generator = section_role == 0
-    with_context = (section_role % 2).astype(jnp.float32)
     rows, _ = latent.shape[1:]
     chunk = rows // lax.axis_size("section")
 
@@ -250,65 +288,76 @@
     )
     w_proj = lax.dynamic_index_in_dim(w_out, (section_role + 1) // 2, 0, keepdims=False)
     inner = w_proj.shape[0]
-    w_wide = jnp.broadcast_to(w_proj[None], (8,) + w_proj.shape)
+    w_there = lax.ppermute(w_proj, "zhi", SWAP)
+    w_swapped = [lax.ppermute(w_proj, "core", SWAP)]
     frame_ids = jnp.where(is_generator, block_ids[0, 0], block_ids[1, 0])
     seen, bounds = visibility(frame_ids)
 
+    w_other = lax.ppermute(w_qkv, "core", SWAP)
+    roles_here = jnp.roll(roles, -section)
+    zhi = lax.axis_index("zhi")
+    ahead = (lax.axis_index("x") + jnp.arange(4, dtype=jnp.int32)) % 4
+    place = jnp.concatenate([roles_here, ahead])
     theirs = lax.ppermute(quarter, "zhi", SWAP)
-    everything = []
-    for ours in (quarter, theirs):
+    pieces, arrived = [], []
+    for i, ours in enumerate((quarter, theirs)):
         left = lax.ppermute(ours, "x", moved("x", 4, 1))
         right = lax.ppermute(ours, "x", moved("x", 4, -1))
         far_scored = lax.ppermute(left[0], "x", moved("x", 4, 1))
         far_latent = lax.ppermute(right[1], "x", moved("x", 4, -1))
-        everything += [ours, right, far_scored, far_latent, left]
-    everything, w_wide = lax.optimization_barrier((everything, w_wide))
-    w_other = lax.ppermute(w_qkv, "core", SWAP)
-    ahead = jnp.arange(4, dtype=jnp.int32)
-    near = (lax.axis_index("x") + ahead) % 4 * 2
-    zhi = lax.axis_index("zhi")
-    place = jnp.concatenate(
-        [jnp.roll(roles, -section), near + zhi, near + (1 - zhi)]
-    )
-    made = project(place, everything, context, w_qkv, w_other)
-    w_mine = lax.all_to_all(w_wide, RING, 0, 0, tiled=True)
-    pieces = [made[0]]
-    for i in range(1, 8):
-        step, side = i // 2, i % 2
-        perm = [
-            (s * 2 + c, (s + step) % 4 * 2 + (c + side) % 2) for s in range(4) for c in range(2)
-        ]
-        pieces.append(lax.ppermute(made[i], ("section", "core"), perm))
-    starts = jnp.arange(8, dtype=jnp.int32)
-    starts = (core + starts) % 2 * 4 + (section - starts // 2) % 4
+        gathered = [ours, right, far_scored, far_latent, left]
+        if i:
+            gathered, w_here, w_there = lax.optimization_barrier((gathered, w_proj, w_there))
+        made = project(place, gathered, context, w_qkv, w_other)
+        for step in (2, 1, 3, 0):
+            for side in range(2):
+                piece = made[2 * step + side]
+                if step or side:
+                    perm = [
+                        (s * 2 + c, (s + step) % 4 * 2 + (c + side) % 2)
+                        for s in range(4)
+                        for c in range(2)
+                    ]
+                    piece = lax.ppermute(piece, ("section", "core"), perm)
+                pieces.append(piece)
+                arrived.append((i, step, side))
+    w_swapped.append(lax.ppermute(w_there, "core", SWAP))
+    left = [lax.ppermute(v, "x", moved("x", 4, 1)) for v in (w_here, w_there)]
+    right = [lax.ppermute(v, "x", moved("x", 4, -1)) for v in (w_here, w_there)]
+    far = [
+        lax.ppermute(left[0], "x", moved("x", 4, 1)),
+        lax.ppermute(right[1], "x", moved("x", 4, -1)),
+    ]
+    near = right + left
+    w_swapped += [lax.ppermute(v, "core", SWAP) for v in near]
+    half, step, side = jnp.array(arrived, jnp.int32).T
+    starts = (zhi + half) % 2 * 8 + (core + side) % 2 * 4 + (section - step) % 4
     attn = attend(pieces, starts, seen, bounds)
-    attn, w_mine = lax.optimization_barrier((attn, w_mine))
-    w_theirs = lax.ppermute(w_mine, "core", SWAP)
     attn = lax.all_to_all(attn.reshape(16, rows, inner), SEQ, 0, 0, tiled=True)
+    w_swapped += [lax.ppermute(v, "core", SWAP) for v in far]
+    w_held = [w_here, w_there] + near + far
+    chips = [(0, 0), (0, 1), (1, 0), (1, 1), (3, 0), (3, 1), (2, 0), (2, 1)]
+    weights, heads = [], []
+    for i, (dx, dz) in enumerate(chips):
+        chip = (lax.axis_index("x") + dx) % 4 * 2 + (zhi + dz) % 2
+        weights += [w_held[i], w_swapped[i]]
+        heads += [chip * 2 + core, chip * 2 + 1 - core]
+    targets = [(section + step) % 4 for step in (2, 1, 3, 0)]
+    block, *terms = finish(
+        jnp.stack(heads + targets + [section_role]), attn, pending[0], latent[0], context, weights
+    )
     attn, stored_attn = lax.optimization_barrier((attn, stored_attn))
     stored = lax.all_to_all(stored_attn.reshape(8, 2 * rows, inner), RING, 0, 0, tiled=True)
-    attn = attn.reshape(8, 2, rows, inner)
-    mine = lax.dynamic_index_in_dim(attn, core, 1, keepdims=False)
-    theirs = lax.dynamic_index_in_dim(attn, 1 - core, 1, keepdims=False)
-    branch = jnp.einsum(
-        "hri,hic->rc", mine, w_mine, preferred_element_type=jnp.float32
-    ) + jnp.einsum("hri,hic->rc", theirs, w_theirs, preferred_element_type=jnp.float32)
-    held = pending[0].astype(jnp.float32) + with_context * context[0][None, :]
-    source = jnp.where(is_generator, latent[0].astype(jnp.float32), held)
-    block_out = (source + branch).astype(jnp.bfloat16)[None, None]
-    return (block_out,) + gradients(own_weight, branch, stored)
-
-
-def gradients(own_weight, branch, stored):
-    rows, width = branch.shape
+    return (block[None, None],) + gradients(terms, stored)
+
+
+def gradients(terms, stored):
+    rows, part = terms[0].shape
+    width = 4 * part
     sections = lax.axis_size("section")
     section, core = lax.axis_index("section"), lax.axis_index("core")
-    part = width // sections
-    terms = (own_weight * branch).astype(jnp.bfloat16)
     total = None
-    for step in (2, 1, 3, 0):
-        column = (section + step) % sections * part
-        term = lax.dynamic_slice_in_dim(terms, column, part, 1)
+    for step, term in zip((2, 1, 3, 0), terms):
         if step:
             term = lax.ppermute(term, "section", moved("section", sections, step))
         total = term.astype(jnp.float32) + (0.0 if total is None else total)

time: 250 us -> 270 us (1.080)
  starting transfers between devices: 61.7 us -> 77.2 us
  Pallas kernels: 44.3 us -> 57.6 us
  matrix products: 10.8 us -> 0.9 us
  between operations: 6.49 us -> 2.45 us
    ppermute x8 -> x29, starting transfers between devices: 8.94 us -> 34.9 us  [the longest x14 18.2 us: per_device(): piece = lax.ppermute(piece, ('section', 'core'), perm)]
    ppermute x8 -> x29, waiting for transfers between devices: 22.8 us -> 10.6 us  [the longest x14 6.86 us: per_device(): piece = lax.ppermute(piece, ('section', 'core'), perm)]
    ppermute x1, waiting for transfers between devices: 1.87 us -> 11.9 us  [per_device(): theirs = lax.ppermute(quarter, 'zhi', SWAP)]
    pallas_call x0 -> x1, Pallas kernels: none -> 9.44 us  [finish(): pl.pallas_call(finish_kernel, out_shape=[jax.ShapeDtypeStruct((rows, widt...]
    dot_general x2 -> x0, matrix products: 8.74 us -> none  [the longest x1 4.93 us: per_device(): jnp.einsum('hri,hic->rc', mine, w_mine, preferred_element_type=jnp.float32)]
    ppermute x2, waiting for transfers between devices: 14.9 us -> 6.13 us  [per_device(): left = lax.ppermute(ours, 'x', moved('x', 4, 1))]
    all_to_all x1 -> x0, starting transfers between devices: 8.68 us -> none  [per_device(): w_mine = lax.all_to_all(w_wide, RING, 0, 0, tiled=True)]
    ppermute x2, waiting for transfers between devices: 4.22 us -> 12.4 us  [per_device(): far_latent = lax.ppermute(right[1], 'x', moved('x', 4, -1))]
  transfers between devices with their start and end apart: 29 -> 49, of which waited for: 18 -> 20; matrix products, arithmetic and copies ran while one was open for 6% -> 8% of each run, Pallas kernels for 18% -> 18%
where the time goes in v3:
time: 270 us; the launch traced here: 267 us
  waiting for transfers between devices  79.4 us (29%)
  starting transfers between devices  77.2 us (29%)
  Pallas kernels  57.6 us (21%)
  blocking collectives  22.4 us (8%)
  local copies, waits for them, and re-layouts  16 us (6%)
  other arithmetic  11.5 us (4%)
    pallas_call x1, Pallas kernels, attend(): pl.pallas_call(attention_kernel, out_shape=jax.ShapeDtypeStruct((length,...  25.2 us
    all_to_all x1, blocking collectives, gradients(): product = lax.all_to_all(product, RING + ('dp',), 0, 0, tiled=True)  22.4 us
    pallas_call x2, Pallas kernels, project(): pl.pallas_call(project_kernel, out_shape=[jax.ShapeDtypeStruct((many, col...  20.2 us
    ppermute x14, starting transfers between devices, per_device(): piece = lax.ppermute(piece, ('section', 'core'), perm)  18.2 us
    ppermute x2, waiting for transfers between devices, per_device(): far_latent = lax.ppermute(right[1], 'x', moved('x', 4, -1))  12.4 us
    ppermute x3, waiting for transfers between devices, gradients(): lax.ppermute(grad_bf, 'section', moved('section', sections, step))  12 us
    ppermute x1, waiting for transfers between devices, per_device(): theirs = lax.ppermute(quarter, 'zhi', SWAP)  11.9 us
    pallas_call x1, Pallas kernels, finish(): pl.pallas_call(finish_kernel, out_shape=[jax.ShapeDtypeStruct((rows, widt...  9.44 us
  transfers between devices with their start and end apart: 49, of which 20 were waited for; matrix products, arithmetic and copies ran while one was open for 8% of the time, Pallas kernels for 18%

profile of v3, /device:TPU:2, one launch (start us, length us, event | category | flops | bytes accessed | tf_op | source)
XLA Modules:
  0.0 267.5 jit_solution(5396874592645785930)
XLA Ops:
  2.0 4.0 %collective-permute-start.12 = (bf16[2,48,2560]{2,1,0:T(8,128)(2,1)S(1)}, bf16[2,48,2560]{2,1,0:T(8,128)(2,1)}, u32[]{:S(2)}, u32[]{:S(2)}) collective-permute-start(bf16[2,48,2560]{2,1,0:T(8,128)(2,1)S(1)} %pad_maximum_fusion.refs_0_), channel_id=1, source_target_pairs={{0,4},{4,0},{1,5},{5,1},{2,6},{6,2},{3,7},{7,3},{8,12},{12,8},{9,1... | collective-permute-start | bytes 1474568 | tf_op jit(solution)/shard_map/ppermute | solution.py:301
  6.0 11.9 %collective-permute-done.12.refs_0_ = bf16[2,48,2560]{2,1,0:T(8,128)(2,1)} collective-permute-done((bf16[2,48,2560]{2,1,0:T(8,128)(2,1)S(1)}, bf16[2,48,2560]{2,1,0:T(8,128)(2,1)}, u32[]{:S(2)}, u32[]{:S(2)}) %collective-permute-start.12) | collective-permute-done | bytes 491552 | tf_op jit(solution)/shard_map/ppermute | solution.py:301
  22.8 3.3 %collective-permute-start.17 = (bf16[128,2560]{1,0:T(8,128)(2,1)S(1)}, bf16[128,2560]{1,0:T(8,128)(2,1)}, u32[]{:S(2)}, u32[]{:S(2)}) collective-permute-start(bf16[128,2560]{1,0:T(8,128)(2,1)S(1)} %dynamic-slice_bitcast_fusion.refs_4_), channel_id=1, source_target_pairs={{0,4},{4,0},{1,5},{5,1},{2,6},{6,2},{3,7},{7,3},{8,12},{12,8},{9,1... | collective-permute-start | bytes 1966088 | tf_op jit(solution)/shard_map/ppermute | solution.py:291
  26.1 6.1 %collective-permute-done.14.refs_4_ = bf16[2,48,2560]{2,1,0:T(8,128)(2,1)} collective-permute-done((bf16[2,48,2560]{2,1,0:T(8,128)(2,1)}, bf16[2,48,2560]{2,1,0:T(8,128)(2,1)}, u32[]{:S(2)}, u32[]{:S(2)}) %collective-permute-start.14) | collective-permute-done | bytes 491552 | tf_op jit(solution)/shard_map/ppermute | solution.py:304
  35.0 8.5 %collective-permute-done.13.refs_1_ = bf16[2,48,2560]{2,1,0:T(8,128)(2,1)S(1)} collective-permute-done((bf16[2,48,2560]{2,1,0:T(8,128)(2,1)}, bf16[2,48,2560]{2,1,0:T(8,128)(2,1)S(1)}, u32[]{:S(2)}, u32[]{:S(2)}) %collective-permute-start.13) | collective-permute-done | bytes 491552 | tf_op jit(solution)/shard_map/ppermute | solution.py:305
  46.6 3.0 %collective-permute-done.15.refs_2_ = bf16[48,2560]{1,0:T(8,128)(2,1)S(1)} collective-permute-done((bf16[48,2560]{1,0:T(8,128)(2,1)S(1)}, bf16[48,2560]{1,0:T(8,128)(2,1)S(1)}, u32[]{:S(2)}, u32[]{:S(2)}) %collective-permute-start.15) | collective-permute-done | bytes 245792 | tf_op jit(solution)/shard_map/ppermute | solution.py:306
  61.4 10.1 %project.3 = (bf16[192,384]{1,0:T(8,128)(2,1)}, bf16[192,384]{1,0:T(8,128)(2,1)}, bf16[192,384]{1,0:T(8,128)(2,1)}, bf16[192,384]{1,0:T(8,128)(2,1)}, bf16[192,3...) custom-call(s32[8]{0:T(128)} %pad_add_fusion.7.place, ...), custom_call_target="tpu_custom_call" | custom-call | tf_op jit(solution)/shard_map/project/pallas_call | solution.py:186
  71.5 3.0 %collective-permute-start.18 = (bf16[192,384]{1,0:T(8,128)(2,1)}, bf16[192,384]{1,0:T(8,128)(2,1)S(1)}, u32[]{:S(2)}, u32[]{:S(2)}) collective-permute-start(bf16[192,384]{1,0:T(8,128)(2,1)} %get-tuple-element.45), channel_id=1, source_target_pairs={{0,64},{2,66},{32,96},{34,98},{64,0},{66,2},{96,32},{98,34},{1,65}... | collective-permute-start | bytes 442376 | tf_op jit(solution)/shard_map/ppermute | solution.py:321
  74.5 10.5 %collective-permute-done.3.refs_3_ = bf16[48,2560]{1,0:T(8,128)(2,1)} collective-permute-done((bf16[48,2560]{1,0:T(8,128)(2,1)}, bf16[48,2560]{1,0:T(8,128)(2,1)}, u32[]{:S(2)}, u32[]{:S(2)}) %collective-permute-start.3) | collective-permute-done | bytes 245792 | tf_op jit(solution)/shard_map/ppermute | solution.py:307
  88.8 10.1 %project.2 = (bf16[192,384]{1,0:T(8,128)(2,1)}, bf16[192,384]{1,0:T(8,128)(2,1)}, bf16[192,384]{1,0:T(8,128)(2,1)}, bf16[192,384]{1,0:T(8,128)(2,1)}, bf16[192,3...) custom-call(s32[8]{0:T(128)} %pad_add_fusion.7.place, ...), custom_call_target="tpu_custom_call" | custom-call | tf_op jit(solution)/shard_map/project/pallas_call | solution.py:186
  98.9 3.0 %collective-permute-start.22 = (bf16[192,384]{1,0:T(8,128)(2,1)}, bf16[192,384]{1,0:T(8,128)(2,1)S(1)}, u32[]{:S(2)}, u32[]{:S(2)}) collective-permute-start(bf16[192,384]{1,0:T(8,128)(2,1)} %get-tuple-element.49), channel_id=1, source_target_pairs={{0,96},{2,98},{32,0},{34,2},{64,32},{66,34},{96,64},{98,66},{1,97}... | collective-permute-start | bytes 442376 | tf_op jit(solution)/shard_map/ppermute | solution.py:321
  106.4 2.9 %collective-permute-start.5 = (bf16[192,384]{1,0:T(8,128)(2,1)}, bf16[192,384]{1,0:T(8,128)(2,1)}, u32[]{:S(2)}, u32[]{:S(2)}) collective-permute-start(bf16[192,384]{1,0:T(8,128)(2,1)} %get-tuple-element.32), channel_id=1, source_target_pairs={{0,64},{2,66},{32,96},{34,98},{64,0},{66,2},{96,32},{98,34},{1,65}... | collective-permute-start | bytes 442376 | tf_op jit(solution)/shard_map/ppermute | solution.py:321
  113.7 4.1 %collective-permute-done.10.refs_5_ = bf16[192,384]{1,0:T(8,128)(2,1)S(1)} collective-permute-done((bf16[192,384]{1,0:T(8,128)(2,1)}, bf16[192,384]{1,0:T(8,128)(2,1)S(1)}, u32[]{:S(2)}, u32[]{:S(2)}) %collective-permute-start.10) | collective-permute-done | bytes 147488 | tf_op jit(solution)/shard_map/ppermute | solution.py:321
  126.5 3.8 %convert_reduce_fusion = s32[3072]{0:T(1024)S(1)} fusion(s32[3072]{0:T(1024)S(1)} %bitcast.85), kind=kLoop, calls=%fused_computation | loop fusion | flops 28308480 | bytes 24576 | tf_op jit(solution)/shard_map/reduce_sum | solution.py:104
  133.9 25.2 %attend.1 = bf16[3072,128]{1,0:T(8,128)(2,1)} custom-call(s32[6,2]{1,0:T(8,128)} %pad_add_fusion.bounds, s32[16]{0:T(128)} %fusion.4.starts, bf16[192,384]{1,0:T(8,128)(2,1)} %collective-permute-done.5.refs_0_, bf16[192,384]{1,0:T(8,128)(2,1)} %collective-permute-done.6.refs_1_, bf16[192,384]{1,0:T(8,128)(2,1)} %collective-permute-done.7.refs_2_, ...), custom_call_target="tpu_custom_call" | custom-call | tf_op jit(solution)/shard_map/attend/pallas_call | solution.py:116
  159.2 7.5 %all-to-all-start = ((bf16[16,192,128]{2,1,0:T(8,128)(2,1)}), bf16[16,192,128]{2,1,0:T(8,128)(2,1)S(1)}, u32[]{:S(2)}, u32[]{:S(2)}) async-start(bf16[16,192,128]{2,1,0:T(8,128)(2,1)} %bitcast.75), calls=%async_computation | async-start | bytes 1572864 | tf_op jit(solution)/shard_map/all_to_all | solution.py:336
  173.0 6.4 %all-to-all-done.refs_0_ = bf16[16,192,128]{2,1,0:T(8,128)(2,1)S(1)} async-done(((bf16[16,192,128]{2,1,0:T(8,128)(2,1)}), bf16[16,192,128]{2,1,0:T(8,128)(2,1)S(1)}, u32[]{:S(2)}, u32[]{:S(2)}) %all-to-all-start) | async-done | bytes 786464 | tf_op jit(solution)/shard_map/all_to_all | solution.py:336
  180.3 9.4 %finish.1 = (bf16[192,2560]{1,0:T(8,128)(2,1)}, bf16[192,640]{1,0:T(8,128)(2,1)}, bf16[192,640]{1,0:T(8,128)(2,1)}, bf16[192,640]{1,0:T(8,128)(2,1)}, bf16[192,640]{1,0:T(8,128)(2,1)}) custom-call(s32[21]{0:T(128)} %stack.147.place, bf16[16,192,128]{2,1,0:T(8,128)(2,1)} %copy-done.1, bf16[192,2560]{1,0:T(8,128)(2,1)} %bitcast.81, ...), custom_call_target="tpu_custom_call" | custom-call | tf_op jit(solution)/shard_map/finish/pallas_call | solution.py:228
  195.9 6.0 %all-to-all-start.1 = ((bf16[8,384,128]{1,2,0:T(8,128)(2,1)}), bf16[8,384,128]{1,2,0:T(8,128)(2,1)S(1)}, u32[]{:S(2)}, u32[]{:S(2)}) async-start(bf16[8,384,128]{1,2,0:T(8,128)(2,1)} %copy.28), calls=%async_computation.1 | async-start | bytes 1572864 | tf_op jit(solution)/shard_map/all_to_all | solution.py:350
  203.2 3.4 %collective-permute-done.40 = bf16[192,640]{1,0:T(8,128)(2,1)} collective-permute-done((bf16[192,640]{1,0:T(8,128)(2,1)}, bf16[192,640]{1,0:T(8,128)(2,1)}, u32[]{:S(2)}, u32[]{:S(2)}) %collective-permute-start.40) | collective-permute-done | bytes 245792 | tf_op jit(solution)/shard_map/ppermute | solution.py:362
  213.9 22.4 %all_to_all.20 = bf16[16,64,640]{2,1,0:T(8,128)(2,1)S(1)} all-to-all(bf16[16,64,640]{2,1,0:T(8,128)(2,1)S(1)} %bitcast.73), channel_id=1, replica_groups=mesh['section'=4,'x'=4,'zhi'=2,'core'=2,'dp'=2] {'x','zhi','dp'}, dimensions={0} | all-to-all | bytes 2621440 | tf_op jit(solution)/shard_map/all_to_all | solution.py:371
  238.9 3.5 %all-to-all-start.3 = ((bf16[8,64,640]{2,1,0:T(8,128)(2,1)}), bf16[8,64,640]{2,1,0:T(8,128)(2,1)S(1)}, u32[]{:S(2)}, u32[]{:S(2)}) async-start(bf16[8,64,640]{2,1,0:T(8,128)(2,1)} %broadcast_in_dim.20), calls=%async_computation.3 | async-start | bytes 1310720 | tf_op jit(solution)/shard_map/all_to_all | solution.py:374
  242.5 3.4 %collective-permute-start.42 = (bf16[192,640]{1,0:T(8,128)(2,1)S(1)}, bf16[192,640]{1,0:T(8,128)(2,1)S(1)}, u32[]{:S(2)}, u32[]{:S(2)}) collective-permute-start(bf16[192,640]{1,0:T(8,128)(2,1)S(1)} %add_convert_fusion.refs_0_), channel_id=1, source_target_pairs={{0,64},{32,96},{64,0},{96,32},{1,65},{33,97},{65,1},{97,33},{2,66}... | collective-permute-start | bytes 737288 | tf_op jit(solution)/shard_map/ppermute | solution.py:379
  249.9 9.4 %collective-permute-done.42.refs_1_ = bf16[192,640]{1,0:T(8,128)(2,1)S(1)} collective-permute-done((bf16[192,640]{1,0:T(8,128)(2,1)S(1)}, bf16[192,640]{1,0:T(8,128)(2,1)S(1)}, u32[]{:S(2)}, u32[]{:S(2)}) %collective-permute-start.42) | collective-permute-done | bytes 245792 | tf_op jit(solution)/shard_map/ppermute | solution.py:379
  (158 shorter events, 83.9 us)
Async XLA Ops:
  0.7 57.9 %collective-permute-start.4 = (bf16[3,2560,384]{2,1,0:T(8,128)(2,1)}, bf16[3,2560,384]{2,1,0:T(8,128)(2,1)}, u32[]{:S(2)}, u32[]{:S(2)}) collective-permute-start(bf16[3,2560,384]{2,1,0:T(8,128)(2,1)} %refs_6_.3), channel_id=1, source_target_pairs={{0,2},{2,0},{1,3},{3,1},{4,6},{6,4},{5,7},{7,5},{8,10},{10,8},{9,1... | collective-permute-start | bytes 17694728 | tf_op jit(solution)/shard_map/ppermute | solution.py:296
  2.0 15.8 %collective-permute-start.12 = (bf16[2,48,2560]{2,1,0:T(8,128)(2,1)S(1)}, bf16[2,48,2560]{2,1,0:T(8,128)(2,1)}, u32[]{:S(2)}, u32[]{:S(2)}) collective-permute-start(bf16[2,48,2560]{2,1,0:T(8,128)(2,1)S(1)} %pad_maximum_fusion.refs_0_), channel_id=1, source_target_pairs={{0,4},{4,0},{1,5},{5,1},{2,6},{6,2},{3,7},{7,3},{8,12},{12,8},{9,1... | collective-permute-start | bytes 1474568 | tf_op jit(solution)/shard_map/ppermute | solution.py:301
  19.4 25.5 %collective-permute-start.1 = (bf16[2,48,2560]{2,1,0:T(8,128)(2,1)S(1)}, bf16[2,48,2560]{2,1,0:T(8,128)(2,1)}, u32[]{:S(2)}, u32[]{:S(2)}) collective-permute-start(bf16[2,48,2560]{2,1,0:T(8,128)(2,1)S(1)} %pad_maximum_fusion.refs_0_), channel_id=1, source_target_pairs={{0,8},{8,16},{16,24},{24,0},{1,9},{9,17},{17,25},{25,1},{2,10},{10... | collective-permute-start | bytes 1474568 | tf_op jit(solution)/shard_map/ppermute | solution.py:304
  20.6 33.1 %collective-permute-start = (bf16[2,48,2560]{2,1,0:T(8,128)(2,1)S(1)}, bf16[2,48,2560]{2,1,0:T(8,128)(2,1)}, u32[]{:S(2)}, u32[]{:S(2)}) collective-permute-start(bf16[2,48,2560]{2,1,0:T(8,128)(2,1)S(1)} %pad_maximum_fusion.refs_0_), channel_id=1, source_target_pairs={{0,24},{8,0},{16,8},{24,16},{1,25},{9,1},{17,9},{25,17},{2,26},{10... | collective-permute-start | bytes 1474568 | tf_op jit(solution)/shard_map/ppermute | solution.py:305
  22.8 23.7 %collective-permute-start.17 = (bf16[128,2560]{1,0:T(8,128)(2,1)S(1)}, bf16[128,2560]{1,0:T(8,128)(2,1)}, u32[]{:S(2)}, u32[]{:S(2)}) collective-permute-start(bf16[128,2560]{1,0:T(8,128)(2,1)S(1)} %dynamic-slice_bitcast_fusion.refs_4_), channel_id=1, source_target_pairs={{0,4},{4,0},{1,5},{5,1},{2,6},{6,2},{3,7},{7,3},{8,12},{12,8},{9,1... | collective-permute-start | bytes 1966088 | tf_op jit(solution)/shard_map/ppermute | solution.py:291
  51.5 33.6 %collective-permute-start.31 = (bf16[128,2560]{1,0:T(8,128)(2,1)S(1)}, bf16[128,2560]{1,0:T(8,128)(2,1)}, u32[]{:S(2)}, u32[]{:S(2)}) collective-permute-start(bf16[128,2560]{1,0:T(8,128)(2,1)S(1)} %dynamic-slice_bitcast_fusion.refs_4_), channel_id=1, source_target_pairs={{0,8},{8,16},{16,24},{24,0},{1,9},{9,17},{17,25},{25,1},{2,10},{10... | collective-permute-start | bytes 1966088 | tf_op jit(solution)/shard_map/ppermute | solution.py:325
  53.7 45.2 %collective-permute-start.27 = (bf16[128,2560]{1,0:T(8,128)(2,1)S(1)}, bf16[128,2560]{1,0:T(8,128)(2,1)}, u32[]{:S(2)}, u32[]{:S(2)}) collective-permute-start(bf16[128,2560]{1,0:T(8,128)(2,1)S(1)} %dynamic-slice_bitcast_fusion.refs_4_), channel_id=1, source_target_pairs={{0,24},{8,0},{16,8},{24,16},{1,25},{9,1},{17,9},{25,17},{2,26},{10... | collective-permute-start | bytes 1966088 | tf_op jit(solution)/shard_map/ppermute | solution.py:326
  53.7 33.0 %collective-permute-start.29 = (bf16[128,2560]{1,0:T(8,128)(2,1)}, bf16[128,2560]{1,0:T(8,128)(2,1)}, u32[]{:S(2)}, u32[]{:S(2)}) collective-permute-start(bf16[128,2560]{1,0:T(8,128)(2,1)} %collective-permute-done.17.refs_6_), channel_id=1, source_target_pairs={{0,24},{8,0},{16,8},{24,16},{1,25},{9,1},{17,9},{25,17},{2,26},{10... | collective-permute-start | bytes 1966088 | tf_op jit(solution)/shard_map/ppermute | solution.py:326
  58.6 26.5 %collective-permute-start.3 = (bf16[48,2560]{1,0:T(8,128)(2,1)}, bf16[48,2560]{1,0:T(8,128)(2,1)}, u32[]{:S(2)}, u32[]{:S(2)}) collective-permute-start(bf16[48,2560]{1,0:T(8,128)(2,1)} %slice_bitcast_fusion.2), channel_id=1, source_target_pairs={{0,24},{8,0},{16,8},{24,16},{1,25},{9,1},{17,9},{25,17},{2,26},{10... | collective-permute-start | bytes 737288 | tf_op jit(solution)/shard_map/ppermute | solution.py:307
  71.5 30.3 %collective-permute-start.18 = (bf16[192,384]{1,0:T(8,128)(2,1)}, bf16[192,384]{1,0:T(8,128)(2,1)S(1)}, u32[]{:S(2)}, u32[]{:S(2)}) collective-permute-start(bf16[192,384]{1,0:T(8,128)(2,1)} %get-tuple-element.45), channel_id=1, source_target_pairs={{0,64},{2,66},{32,96},{34,98},{64,0},{66,2},{96,32},{98,34},{1,65}... | collective-permute-start | bytes 442376 | tf_op jit(solution)/shard_map/ppermute | solution.py:321
  85.1 16.8 %collective-permute-start.19 = (bf16[192,384]{1,0:T(8,128)(2,1)}, bf16[192,384]{1,0:T(8,128)(2,1)S(1)}, u32[]{:S(2)}, u32[]{:S(2)}) collective-permute-start(bf16[192,384]{1,0:T(8,128)(2,1)} %get-tuple-element.46), channel_id=1, source_target_pairs={{0,66},{2,64},{32,98},{34,96},{64,2},{66,0},{96,34},{98,32},{1,67}... | collective-permute-start | bytes 442376 | tf_op jit(solution)/shard_map/ppermute | solution.py:321
  85.1 18.0 %collective-permute-start.20 = (bf16[192,384]{1,0:T(8,128)(2,1)}, bf16[192,384]{1,0:T(8,128)(2,1)S(1)}, u32[]{:S(2)}, u32[]{:S(2)}) collective-permute-start(bf16[192,384]{1,0:T(8,128)(2,1)} %get-tuple-element.47), channel_id=1, source_target_pairs={{0,32},{2,34},{32,64},{34,66},{64,96},{66,98},{96,0},{98,2},{1,33}... | collective-permute-start | bytes 442376 | tf_op jit(solution)/shard_map/ppermute | solution.py:321
  86.7 16.5 %collective-permute-start.21 = (bf16[192,384]{1,0:T(8,128)(2,1)}, bf16[192,384]{1,0:T(8,128)(2,1)S(1)}, u32[]{:S(2)}, u32[]{:S(2)}) collective-permute-start(bf16[192,384]{1,0:T(8,128)(2,1)} %get-tuple-element.48), channel_id=1, source_target_pairs={{0,34},{2,32},{32,66},{34,64},{64,98},{66,96},{96,2},{98,0},{1,35}... | collective-permute-start | bytes 442376 | tf_op jit(solution)/shard_map/ppermute | solution.py:321
  118.7 48.0 %collective-permute-start.33 = (bf16[128,2560]{1,0:T(8,128)(2,1)}, bf16[128,2560]{1,0:T(8,128)(2,1)S(1)}, u32[]{:S(2)}, u32[]{:S(2)}) collective-permute-start(bf16[128,2560]{1,0:T(8,128)(2,1)} %collective-permute-done.17.refs_6_), channel_id=1, source_target_pairs={{0,8},{8,16},{16,24},{24,0},{1,9},{9,17},{17,25},{25,1},{2,10},{10... | collective-permute-start | bytes 1966088 | tf_op jit(solution)/shard_map/ppermute | solution.py:325
  120.7 46.2 %collective-permute-start.26 = (bf16[128,2560]{1,0:T(8,128)(2,1)}, bf16[128,2560]{1,0:T(8,128)(2,1)}, u32[]{:S(2)}, u32[]{:S(2)}) collective-permute-start(bf16[128,2560]{1,0:T(8,128)(2,1)} %collective-permute-done.17.refs_6_), channel_id=1, source_target_pairs={{0,2},{2,0},{1,3},{3,1},{4,6},{6,4},{5,7},{7,5},{8,10},{10,8},{9,1... | collective-permute-start | bytes 1966088 | tf_op jit(solution)/shard_map/ppermute | solution.py:324
  123.5 43.8 %collective-permute-start.35 = (bf16[128,2560]{1,0:T(8,128)(2,1)}, bf16[128,2560]{1,0:T(8,128)(2,1)}, u32[]{:S(2)}, u32[]{:S(2)}) collective-permute-start(bf16[128,2560]{1,0:T(8,128)(2,1)} %collective-permute-done.31.refs_12_), channel_id=1, source_target_pairs={{0,8},{8,16},{16,24},{24,0},{1,9},{9,17},{17,25},{25,1},{2,10},{10... | collective-permute-start | bytes 1966088 | tf_op jit(solution)/shard_map/ppermute | solution.py:328
  126.4 41.1 %collective-permute-start.37 = (bf16[128,2560]{1,0:T(8,128)(2,1)}, bf16[128,2560]{1,0:T(8,128)(2,1)}, u32[]{:S(2)}, u32[]{:S(2)}) collective-permute-start(bf16[128,2560]{1,0:T(8,128)(2,1)} %collective-permute-done.29.refs_10_), channel_id=1, source_target_pairs={{0,24},{8,0},{16,8},{24,16},{1,25},{9,1},{17,9},{25,17},{2,26},{10... | collective-permute-start | bytes 1966088 | tf_op jit(solution)/shard_map/ppermute | solution.py:329
  126.4 41.5 %collective-permute-start.28 = (bf16[128,2560]{1,0:T(8,128)(2,1)}, bf16[128,2560]{1,0:T(8,128)(2,1)}, u32[]{:S(2)}, u32[]{:S(2)}) collective-permute-start(bf16[128,2560]{1,0:T(8,128)(2,1)} %collective-permute-done.27.refs_8_), channel_id=1, source_target_pairs={{0,2},{2,0},{1,3},{3,1},{4,6},{6,4},{5,7},{7,5},{8,10},{10,8},{9,1... | collective-permute-start | bytes 1966088 | tf_op jit(solution)/shard_map/ppermute | solution.py:332
  159.2 20.3 %all-to-all-start = ((bf16[16,192,128]{2,1,0:T(8,128)(2,1)}), bf16[16,192,128]{2,1,0:T(8,128)(2,1)S(1)}, u32[]{:S(2)}, u32[]{:S(2)}) async-start(bf16[16,192,128]{2,1,0:T(8,128)(2,1)} %bitcast.75), calls=%async_computation | async-start | bytes 1572864 | tf_op jit(solution)/shard_map/all_to_all | solution.py:336
  195.9 17.1 %all-to-all-start.1 = ((bf16[8,384,128]{1,2,0:T(8,128)(2,1)}), bf16[8,384,128]{1,2,0:T(8,128)(2,1)S(1)}, u32[]{:S(2)}, u32[]{:S(2)}) async-start(bf16[8,384,128]{1,2,0:T(8,128)(2,1)} %copy.28), calls=%async_computation.1 | async-start | bytes 1572864 | tf_op jit(solution)/shard_map/all_to_all | solution.py:350
  238.9 26.5 %all-to-all-start.3 = ((bf16[8,64,640]{2,1,0:T(8,128)(2,1)}), bf16[8,64,640]{2,1,0:T(8,128)(2,1)S(1)}, u32[]{:S(2)}, u32[]{:S(2)}) async-start(bf16[8,64,640]{2,1,0:T(8,128)(2,1)} %broadcast_in_dim.20), calls=%async_computation.3 | async-start | bytes 1310720 | tf_op jit(solution)/shard_map/all_to_all | solution.py:374
  242.5 16.8 %collective-permute-start.42 = (bf16[192,640]{1,0:T(8,128)(2,1)S(1)}, bf16[192,640]{1,0:T(8,128)(2,1)S(1)}, u32[]{:S(2)}, u32[]{:S(2)}) collective-permute-start(bf16[192,640]{1,0:T(8,128)(2,1)S(1)} %add_convert_fusion.refs_0_), channel_id=1, source_target_pairs={{0,64},{32,96},{64,0},{96,32},{1,65},{33,97},{65,1},{97,33},{2,66}... | collective-permute-start | bytes 737288 | tf_op jit(solution)/shard_map/ppermute | solution.py:379
  245.9 16.0 %collective-permute-start.43 = (bf16[192,640]{1,0:T(8,128)(2,1)S(1)}, bf16[192,640]{1,0:T(8,128)(2,1)S(1)}, u32[]{:S(2)}, u32[]{:S(2)}) collective-permute-start(bf16[192,640]{1,0:T(8,128)(2,1)S(1)} %add_convert_fusion.refs_0_), channel_id=1, source_target_pairs={{0,32},{32,64},{64,96},{96,0},{1,33},{33,65},{65,97},{97,1},{2,34}... | collective-permute-start | bytes 737288 | tf_op jit(solution)/shard_map/ppermute | solution.py:379
  246.5 15.5 %collective-permute-start.44 = (bf16[192,640]{1,0:T(8,128)(2,1)S(1)}, bf16[192,640]{1,0:T(8,128)(2,1)}, u32[]{:S(2)}, u32[]{:S(2)}) collective-permute-start(bf16[192,640]{1,0:T(8,128)(2,1)S(1)} %add_convert_fusion.refs_0_), channel_id=1, source_target_pairs={{0,96},{32,0},{64,32},{96,64},{1,97},{33,1},{65,33},{97,65},{2,98}... | collective-permute-start | bytes 737288 | tf_op jit(solution)/shard_map/ppermute | solution.py:379
  (48 other events, 683.5 us)
